TPU v7x, 32 devices: a whole 2x2x4 slice. The times are simulated.
32 devices in a mesh: seq: 16 (over z, x, core), wshard: 2 (over y).
Axes of the slice: x: 2, y: 2, z: 4, core: 2. Of those that a mesh axis runs over, the one named last changes fastest.
Arguments:
- inputs: float32 [2, 4096, 768], P('wshard', 'seq'), may hold values from -6 to 6
- lengths: int32 [2], P('wshard'), may hold values from 1024 to 4096, as said below
- cotangent: float32 [2, 4096, 768], P('wshard', 'seq'), may hold values from -6 to 6
- query_weight: float32 [768, 768], P('wshard'), may hold values from -0.21875 to 0.21875
- query_bias: float32 [768], P('wshard'), may hold values from -2 to 2
- key_weight: float32 [768, 768], P('wshard'), may hold values from -0.21875 to 0.21875
- value_weight: float32 [768, 768], P('wshard'), may hold values from -0.21875 to 0.21875
- value_bias: float32 [768], P('wshard'), may hold values from -2 to 2
- output_weight: float32 [768, 768], P('wshard'), may hold values from -6 to 6
- output_bias: float32 [768], P('wshard'), may hold values from -2 to 2
- first_gain: float32 [768], P('wshard'), may hold values from 0.25 to 1.75
- first_shift: float32 [768], P('wshard'), may hold values from -2 to 2
- up_weight: float32 [768, 3072], P('wshard'), may hold values from -0.21875 to 0.21875
- up_bias: float32 [3072], P('wshard'), may hold values from -2 to 2
- down_weight: float32 [3072, 768], P('wshard'), may hold values from -0.109375 to 0.109375
- down_bias: float32 [768], P('wshard'), may hold values from -2 to 2
- second_gain: float32 [768], P('wshard'), may hold values from 0.25 to 1.75
- second_shift: float32 [768], P('wshard'), may hold values from -2 to 2
Outputs:
- outputs: float32 [2, 4096, 768], P('wshard', 'seq')
- input_grad: float32 [2, 4096, 768], P('wshard', 'seq')
- grad_query_weight: float32 [768, 768], P('wshard')
- grad_query_bias: float32 [768], P('wshard')
- grad_key_weight: float32 [768, 768], P('wshard')
- grad_value_weight: float32 [768, 768], P('wshard')
- grad_value_bias: float32 [768], P('wshard')
- grad_output_weight: float32 [768, 768], P('wshard')
- grad_output_bias: float32 [768], P('wshard')
- grad_first_gain: float32 [768], P('wshard')
- grad_first_shift: float32 [768], P('wshard')
- grad_up_weight: float32 [768, 3072], P('wshard')
- grad_up_bias: float32 [3072], P('wshard')
- grad_down_weight: float32 [3072, 768], P('wshard')
- grad_down_bias: float32 [768], P('wshard')
- grad_second_gain: float32 [768], P('wshard')
- grad_second_shift: float32 [768], P('wshard')
Inputs may be any that keep to these rules, and one draw needn't show every extreme that they name: `lengths`: some sequence has all 4096 positions valid in every draw.
All inputs are finite; a program needn't handle non-finite values.
Results may differ from a plain program's by a relative error of at most 0.024.
Values may be sent and summed in bfloat16 or wider, within the bound.
No kernel may reach another device: no remote copies, remote signals or barrier semaphores. Data moves between devices by JAX's collectives and lax.ppermute only.
A program may use at most 256 MiB of HBM per device.

v0:
```python
from functools import partial

import jax
import jax.numpy as jnp
from jax import lax
from jax.experimental import pallas as pl
from jax.experimental.pallas import tpu as pltpu
from jax.sharding import Mesh, PartitionSpec as P

HEADS = 12
ZS = 4
NEG_FILL = -1e30
VMEM_LIMIT = 60 << 20
SWAP = ((0, 1), (1, 0))
F32 = jnp.float32
BF16 = jnp.bfloat16


def matmul(left_side, right_side):
    return jnp.dot(left_side, right_side, preferred_element_type=F32)


def right_trans(left_side, right_side):
    return lax.dot_general(
        left_side, right_side, (((1,), (1,)), ((), ())), preferred_element_type=F32
    )


def work(units):
    return pl.CostEstimate(flops=int(units * 1e3), bytes_accessed=1, transcendentals=0)


def swap(value, axis):
    return lax.ppermute(value, axis, SWAP)


def touched_groups(length, rows, outer):
    group = 4 * rows
    left = length - outer * (ZS * group)
    return jnp.clip((left + group - 1) // group, 0, ZS)


def with_mask(kv, place, length):
    at = place + lax.broadcasted_iota(jnp.int32, kv.shape, 0)
    lane = lax.broadcasted_iota(jnp.int32, kv.shape, 1)
    fill = jnp.where(at < length, 0.0, jnp.where(lane == 0, NEG_FILL, 0.0))
    return jnp.concatenate([kv, fill.astype(BF16)], axis=1)


def load_head(kv_refs, rows_ref, turned_ref, low):
    head_dim = turned_ref.shape[1]
    for at, ref in enumerate(kv_refs):
        block, half = at // 2, at % 2
        size = ref.shape[0]
        for start in range(0, size, 256):
            value = ref[start : start + 256, :]
            place = slice(half * size + start, half * size + start + 256)
            rows_ref[block, place, :] = value
            turned_ref[block, :, place] = value.T[low : low + head_dim, :]


def forward_kernel(meta_ref, *refs, blocks, rows):
    query_refs, kv_refs = refs[:2], refs[2 : 2 + 2 * blocks]
    out_ref, *refs = refs[2 + 2 * blocks :]
    piece_refs, (log_ref, rows_ref, turned_ref) = refs[:ZS], refs[ZS:]
    head_dim, query_count = out_ref.shape
    length, z_at = meta_ref[0], meta_ref[1]
    load_head(kv_refs, rows_ref, turned_ref, head_dim)
    query = jnp.concatenate([ref[...] for ref in query_refs], axis=1)
    query = jnp.concatenate(
        [
            query,
            jnp.zeros((head_dim, query_count), BF16),
            jnp.ones((128, query_count), BF16),
        ],
        axis=0,
    )

    def step(group, carry, members):
        top, total, acc = carry
        start = pl.multiple_of((group ^ z_at) * rows, rows)
        found = []
        for block in members:
            place = (meta_ref[2 + block] + group * 4) * rows
            kv = with_mask(rows_ref[block, pl.ds(start, rows), :], place, length)
            found.append(matmul(kv, query))
        new_top = top
        for scores in found:
            new_top = jnp.maximum(new_top, jnp.max(scores, axis=0, keepdims=True))
        fade = jnp.exp(top - new_top)
        total = total * fade
        acc = acc * fade
        for block, scores in zip(members, found):
            weights = jnp.exp(scores - new_top)
            total = total + jnp.sum(weights, axis=0, keepdims=True)
            acc = acc + matmul(
                turned_ref[block, :, pl.ds(start, rows)], weights.astype(BF16)
            )
        return new_top, total, acc

    carry = (
        jnp.full((1, query_count), NEG_FILL, F32),
        jnp.zeros((1, query_count), F32),
        jnp.zeros((head_dim, query_count), F32),
    )
    for first in range(0, blocks, 4):
        members = tuple(range(first, first + 4))
        count = touched_groups(length, rows, meta_ref[2 + first] // 16)
        carry = lax.fori_loop(0, count, lambda g, c: step(g, c, members), carry)
    top, total, acc = carry
    out = acc * (1.0 / total)
    out_ref[...] = out
    size = query_count // ZS
    for at in range(ZS):
        piece_refs[at][...] = out[:, at * size : (at + 1) * size].astype(BF16)
    log_ref[0] = top + jnp.log(total)


def attend_forward(meta, queries, kv_blocks, heads):
    blocks = len(kv_blocks)
    half_rows = kv_blocks[0][0].shape[0]
    part, half_count = queries[0].shape
    head_dim, query_count = part // heads, 2 * half_count
    size = query_count // ZS
    return pl.pallas_call(
        partial(forward_kernel, blocks=blocks, rows=2 * half_rows // ZS),
        grid_spec=pltpu.PrefetchScalarGridSpec(
            num_scalar_prefetch=1,
            grid=(heads,),
            in_specs=[pl.BlockSpec((head_dim, half_count), lambda i, m: (i, 0))] * 2
            + [pl.BlockSpec((half_rows, 128), lambda i, m: (0, i))] * (2 * blocks),
            out_specs=[pl.BlockSpec((head_dim, query_count), lambda i, m: (i, 0))]
            + [pl.BlockSpec((head_dim, size), lambda i, m: (i, 0))] * ZS
            + [pl.BlockSpec((1, 1, query_count), lambda i, m: (i, 0, 0))],
            scratch_shapes=[
                pltpu.VMEM((blocks, 2 * half_rows, 128), BF16),
                pltpu.VMEM((blocks, head_dim, 2 * half_rows), BF16),
            ],
        ),
        out_shape=[jax.ShapeDtypeStruct((part, query_count), F32)]
        + [jax.ShapeDtypeStruct((part, size), BF16)] * ZS
        + [jax.ShapeDtypeStruct((heads, 1, query_count), F32)],
        compiler_params=pltpu.CompilerParams(vmem_limit_bytes=VMEM_LIMIT),
        cost_estimate=work(8 * heads),
        name="attend_forward",
    )(meta, *queries, *[item for pair in kv_blocks for item in pair])


def backward_kernel(meta_ref, *refs, blocks, rows, extra):
    query_refs, (out_ref, log_ref), refs = refs[:2], refs[2:4], refs[4:]
    grad_refs, kv_refs = refs[:ZS], refs[ZS : ZS + 2 * blocks]
    refs = refs[ZS + 2 * blocks + extra :]
    dq_refs, pairs = refs[:ZS], refs[ZS : ZS + blocks // 2]
    rows_ref, turned_ref, qn_ref, gn_ref, acc_ref = refs[ZS + blocks // 2 :]
    head_dim, query_count = out_ref.shape
    length, z_at = meta_ref[0], meta_ref[1]
    block_rows = ZS * rows
    load_head(kv_refs, rows_ref, turned_ref, 0)
    query = jnp.concatenate([ref[...] for ref in query_refs], axis=1)
    grads = jnp.concatenate([ref[...] for ref in grad_refs], axis=1)
    blank = jnp.zeros((head_dim, query_count), BF16)
    query = jnp.concatenate([query, blank], axis=0)
    grad = jnp.concatenate([blank, grads], axis=0)
    qn_ref[...] = query.T
    gn_ref[...] = grad.T
    query = jnp.concatenate([query, jnp.ones((128, query_count), BF16)], axis=0)
    delta = jnp.sum(grads.astype(F32) * out_ref[...], axis=0, keepdims=True)
    log_sum = log_ref[0]
    acc_ref[...] = jnp.zeros_like(acc_ref)

    def put(block, start, value):
        pairs[block // 2][pl.ds(start + (block & 1) * block_rows, rows), :] = value

    def step(group, members):
        start = pl.multiple_of((group ^ z_at) * rows, rows)
        for block in members:
            kv = rows_ref[block, pl.ds(start, rows), :]
            place = (meta_ref[2 + block] + group * 4) * rows
            scores = matmul(with_mask(kv, place, length), query)
            prob_grad = matmul(kv, grad)
            prob = jnp.exp(scores - log_sum)
            score_grad = (prob * (prob_grad - delta)).astype(BF16)
            value = matmul(prob.astype(BF16), gn_ref[...]) + matmul(score_grad, qn_ref[...])
            put(block, start, value.astype(BF16))
            acc_ref[...] += matmul(turned_ref[block, :, pl.ds(start, rows)], score_grad)

    def clear(group, members):
        start = pl.multiple_of((group ^ z_at) * rows, rows)
        for block in members:
            put(block, start, jnp.zeros((rows, 128), BF16))

    def loop(low, high, fn):
        def one(group, carry):
            fn(group)
            return carry

        lax.fori_loop(low, high, one, 0)

    for first in range(0, blocks, 4):
        members = tuple(range(first, first + 4))
        count = touched_groups(length, rows, meta_ref[2 + first] // 16)
        loop(0, count, lambda g: step(g, members))
        loop(count, ZS, lambda g: clear(g, members))
    dq = (acc_ref[...] * head_dim ** (-0.5)).astype(BF16)
    size = query_count // ZS
    for at in range(ZS):
        dq_refs[at][...] = dq[:, at * size : (at + 1) * size]


def attend_backward(meta, queries, grads, out, log_sum, kv_blocks, first, count, made=()):
    blocks = len(kv_blocks)
    half_rows, columns = kv_blocks[0][0].shape
    heads = columns // 128
    part, half_count = queries[0].shape
    head_dim, query_count = part // heads, 2 * half_count
    size = query_count // ZS
    piece = pl.BlockSpec((head_dim, size), lambda i, m: (i + first, 0))
    ins = [
        *queries,
        out,
        log_sum,
        *grads,
        *[item for pair in kv_blocks for item in pair],
        *made,
    ]
    return pl.pallas_call(
        partial(backward_kernel, blocks=blocks, rows=2 * half_rows // ZS, extra=len(made)),
        grid_spec=pltpu.PrefetchScalarGridSpec(
            num_scalar_prefetch=1,
            grid=(count,),
            in_specs=[pl.BlockSpec((head_dim, half_count), lambda i, m: (i + first, 0))] * 2
            + [
                pl.BlockSpec((head_dim, query_count), lambda i, m: (i + first, 0)),
                pl.BlockSpec((1, 1, query_count), lambda i, m: (i + first, 0, 0)),
            ]
            + [piece] * ZS
            + [pl.BlockSpec((half_rows, 128), lambda i, m: (0, i + first))] * (2 * blocks)
            + [pl.BlockSpec(memory_space=pl.ANY)] * len(made),
            out_specs=[piece] * ZS
            + [pl.BlockSpec((4 * half_rows, 128), lambda i, m: (0, i + first))] * (blocks // 2),
            scratch_shapes=[
                pltpu.VMEM((blocks, 2 * half_rows, 128), BF16),
                pltpu.VMEM((blocks, head_dim, 2 * half_rows), BF16),
                pltpu.VMEM((query_count, 128), BF16),
                pltpu.VMEM((query_count, 128), BF16),
                pltpu.VMEM((head_dim, query_count), F32),
            ],
        ),
        out_shape=[jax.ShapeDtypeStruct((part, size), BF16)] * ZS
        + [jax.ShapeDtypeStruct((4 * half_rows, columns), BF16)] * (blocks // 2),
        input_output_aliases={
            1 + len(ins) - len(made) + at: at for at in range(len(made))
        },
        compiler_params=pltpu.CompilerParams(vmem_limit_bytes=VMEM_LIMIT),
        cost_estimate=work(12 * count),
        name="attend_backward",
    )(meta, *ins)


IN_VMEM = pl.BlockSpec(memory_space=pltpu.VMEM)


def small_call(kernel, meta, values, shapes, scratch=(), limit=32, name=None):
    return pl.pallas_call(
        kernel,
        grid_spec=pltpu.PrefetchScalarGridSpec(
            num_scalar_prefetch=1,
            grid=(),
            in_specs=[IN_VMEM] * len(values),
            out_specs=[IN_VMEM] * len(shapes),
            scratch_shapes=list(scratch),
        ),
        out_shape=[jax.ShapeDtypeStruct(shape, kind) for shape, kind in shapes],
        compiler_params=pltpu.CompilerParams(vmem_limit_bytes=limit << 20),
        cost_estimate=work(1),
        name=name,
    )(meta, *values)


def fold_kernel(meta_ref, kept_ref, got_ref, keep_ref, sent_ref, sum_ref):
    sum_ref[...] = (kept_ref[...].astype(F32) + got_ref[...].astype(F32)).astype(BF16)
    rows = keep_ref.shape[0]
    for at, ref in enumerate((keep_ref, sent_ref)):
        start = pl.multiple_of((meta_ref[0] ^ at) * rows, 16)
        ref[...] = sum_ref[pl.ds(start, rows), :]


def fold(bit, kept, got):
    rows, columns = kept.shape
    half = ((rows // 2, columns), BF16)
    return small_call(
        fold_kernel,
        bit,
        (kept, got),
        [half, half],
        [pltpu.VMEM((rows, columns), BF16)],
        name="fold",
    )


def unite_kernel(meta_ref, own_ref, got_ref, out_ref):
    rows = own_ref.shape[0]
    for at, ref in enumerate((own_ref, got_ref)):
        start = pl.multiple_of((meta_ref[0] ^ at) * rows, 16)
        out_ref[pl.ds(start, rows), :] = ref[...]


def unite(bit, own, got):
    rows, columns = own.shape
    return small_call(
        unite_kernel, bit, (own, got), [((2 * rows, columns), BF16)], name="unite"
    )[0]


def plus_kernel(meta_ref, one_ref, two_ref, out_ref, *, low):
    cut = slice(low, low + out_ref.shape[0])
    out_ref[...] = (one_ref[cut, :].astype(F32) + two_ref[cut, :].astype(F32)).astype(BF16)


def plus(meta, one, two, low=0):
    rows, columns = one.shape
    return small_call(
        partial(plus_kernel, low=low),
        meta,
        (one, two),
        [((rows - low, columns), BF16)],
        name="plus",
    )[0]


def prepare_kernel(meta_ref, *refs):
    sources, refs = refs[:3], refs[3:]
    kv_ref, query_ref, low_refs, head_ref = refs[0], refs[1], refs[2:5], refs[5]
    places, sems = refs[6:9], refs[9]
    copies = []
    for at in range(3):
        copies.append(pltpu.make_async_copy(sources[at], places[at], sems.at[at]))
        copies[-1].start()
    z_at, c_at = meta_ref[0], meta_ref[1]
    width = places[0].shape[1]
    part = width // ZS
    head_dim = width // HEADS
    parts = []
    for kind in range(3):
        ref = places[kind]
        copies[kind].wait()
        value = ref[...]
        low_refs[kind][...] = value.astype(BF16)
        half = ref.shape[0] // 2
        rows = ref[pl.ds(pl.multiple_of(c_at * half, half), half), :]
        head_ref[kind * half : (kind + 1) * half, :] = rows.astype(BF16)
        turn = lax.rem(width - z_at * part, width)
        parts.append(pltpu.roll(value, turn, 1)[:, :part])
    columns = []
    for head in range(part // head_dim):
        cut = slice(head * head_dim, (head + 1) * head_dim)
        columns += [parts[1][:, cut], parts[2][:, cut]]
    kv_ref[...] = jnp.concatenate(columns, axis=1).astype(BF16)
    query_ref[...] = parts[0].astype(BF16)


def prepare(meta, weights):
    count, width = weights[0].shape
    shapes = [(count, 2 * width // ZS), (count, width // ZS)] + [(count, width)] * 3
    shapes.append((3 * count // 2, width))
    return pl.pallas_call(
        prepare_kernel,
        grid_spec=pltpu.PrefetchScalarGridSpec(
            num_scalar_prefetch=1,
            grid=(),
            in_specs=[pl.BlockSpec(memory_space=pltpu.MemorySpace.HBM)] * 3,
            out_specs=[IN_VMEM] * len(shapes),
            scratch_shapes=[pltpu.VMEM((count, width), F32)] * 3
            + [pltpu.SemaphoreType.DMA((3,))],
        ),
        out_shape=[jax.ShapeDtypeStruct(shape, BF16) for shape in shapes],
        compiler_params=pltpu.CompilerParams(vmem_limit_bytes=VMEM_LIMIT),
        cost_estimate=work(1),
        name="prepare",
    )(meta, *weights)


def round_kernel(meta_ref, out_w, up_w, down_w, low_out, low_up, low_down, pack_ref):
    core = meta_ref[1]
    for source, target in ((out_w, low_out), (up_w, low_up), (down_w, low_down)):
        target[...] = source[...].astype(BF16)
    width = pack_ref.shape[1]
    low = 0
    half = out_w.shape[0] // 2
    rows = pl.ds(pl.multiple_of(core * half, half), half)
    pack_ref[low : low + half, :] = out_w[rows, :].astype(BF16)
    low += half
    count = up_w.shape[1] // 2
    for block in range(count // width):
        lanes = pl.ds(pl.multiple_of(core * count + block * width, 128), width)
        pack_ref[low : low + up_w.shape[0], :] = up_w[:, lanes].astype(BF16)
        low += up_w.shape[0]
    half = down_w.shape[0] // 2
    rows = pl.ds(pl.multiple_of(core * half, half), half)
    pack_ref[low : low + half, :] = down_w[rows, :].astype(BF16)


def round_weights(meta, weights):
    out_w, up_w, down_w = weights
    width = out_w.shape[1]
    total = out_w.shape[0] // 2 + up_w.shape[0] * (up_w.shape[1] // 2 // width)
    total += down_w.shape[0] // 2
    return small_call(
        round_kernel,
        meta,
        weights,
        [(item.shape, BF16) for item in weights] + [((total, width), BF16)],
        limit=60,
        name="round_weights",
    )


def project_kernel(meta_ref, first_ref, second_ref, *refs, shared):
    query_ref, kv_ref, turned_ref, token_ref, bias_ref = refs[-5:]
    part = query_ref.shape[0]
    rows, width = first_ref.shape
    split = 2 * part
    token_ref[:rows, :] = first_ref[...]
    token_ref[rows:, :] = second_ref[...]
    if shared:
        w_at, z_at = meta_ref[0], meta_ref[1]
        both = None
        bias_ref[...] = jnp.zeros_like(bias_ref)
        for at in range(2):
            count = refs[at].shape[0]
            cut = pl.ds(pl.multiple_of((w_at ^ at) * count, 128), count)
            tokens = token_ref[:, cut]
            terms = [matmul(tokens, refs[2 * at + kind][...]) for kind in range(2)]
            term = jnp.concatenate(terms, axis=1)
            both = term if both is None else both + term
            bias_ref[0:2, cut] = refs[4 + at][0:2, :].astype(F32)
        turn = lax.rem(width - z_at * part, width)
        bias = pltpu.roll(bias_ref[...], turn, 1)[:, :part]
        head_dim = width // HEADS
        pieces = []
        for head in range(part // head_dim):
            pieces.append(jnp.zeros((1, head_dim), F32))
            pieces.append(bias[1:2, head * head_dim : (head + 1) * head_dim])
        both = both + jnp.concatenate(pieces + [bias[0:1, :]], axis=1)
    else:
        both = matmul(token_ref[...], refs[0][...]) + refs[1][...]
    kv_ref[...] = both[:, :split].astype(BF16)
    scale = (part * ZS // HEADS) ** (-0.5)
    query_ref[...] = (both[:, split:].astype(BF16) * jnp.array(scale, BF16)).T
    turned_ref[...] = token_ref[...].T


def project(meta, first, second, sources):
    rows, width = first.shape
    part = width // ZS
    return small_call(
        partial(project_kernel, shared=len(sources) == 6),
        meta,
        (first, second, *sources),
        [((part, 2 * rows), BF16), ((2 * rows, 2 * part), BF16), ((width, 2 * rows), BF16)],
        [pltpu.VMEM((2 * rows, width), BF16), pltpu.VMEM((8, width), F32)],
        limit=40,
        name="project",
    )


def middle_kernel(meta_ref, tokens_ref, seed_ref, vec_ref, upoff_ref, *refs, groups, shared):
    mixed_refs = [refs[at * ZS : (at + 1) * ZS] for at in range(len(groups))]
    refs = refs[ZS * len(groups) :]
    weight_refs = refs[: 5 if shared else 3]
    refs = refs[len(weight_refs) :]
    outputs_ref, resid_ref = refs[:2]
    mgrad_refs = refs[2 : 2 + ZS]
    (
        send_ref,
        keep_ref,
        small_ref,
        out_w,
        up_w,
        down_w,
        slope_ref,
        wide_ref,
        tall_ref,
        sems,
    ) = refs[2 + ZS :]
    w_at, core, z_at = meta_ref[1], meta_ref[2], meta_ref[3]
    moves = [[], [], []]
    if shared:
        outs, ups, downs, got, pair = weight_refs
        count_o, count_u, count_d = outs.shape[0], ups.shape[0], downs.shape[0]
        for kind, (source, target) in enumerate(((outs, out_w), (ups, up_w), (downs, down_w))):
            start = pl.multiple_of(w_at * source.shape[0], source.shape[0])
            moves[kind].append((source, target.at[pl.ds(start, source.shape[0]), :]))
        lanes = got.shape[1]
        for source, which in ((got, core), (pair, 1 - core)):
            half = count_o // 2
            start = pl.multiple_of(((1 - w_at) * 2 + which) * half, half)
            moves[0].append((source.at[pl.ds(0, half), :], out_w.at[pl.ds(start, half), :]))
            low = half
            start = pl.multiple_of((1 - w_at) * count_u, count_u)
            for block in range(up_w.shape[1] // 2 // lanes):
                lane = pl.multiple_of(which * (up_w.shape[1] // 2) + block * lanes, 128)
                moves[1].append(
                    (
                        source.at[pl.ds(low, count_u), :],
                        up_w.at[pl.ds(start, count_u), pl.ds(lane, lanes)],
                    )
                )
                low += count_u
            half = count_d // 2
            start = pl.multiple_of(((1 - w_at) * 2 + which) * half, half)
            moves[2].append((source.at[pl.ds(low, half), :], down_w.at[pl.ds(start, half), :]))
    else:
        for kind, pair in enumerate(zip(weight_refs, (out_w, up_w, down_w))):
            moves[kind].append(pair)
    copies = []
    at = 0
    for kind in range(3):
        made = []
        for source, target in moves[kind]:
            made.append(pltpu.make_async_copy(source, target, sems.at[at]))
            made[-1].start()
            at += 1
        copies.append(made)
    rows, width = tokens_ref.shape
    hidden = upoff_ref.shape[1]
    part = width // ZS
    head_dim = width // HEADS
    quarter = hidden // 4

    def mean(value):
        return jnp.mean(value, axis=-1, keepdims=True)

    def norm(value):
        centered = value - mean(value)
        scale = lax.rsqrt(mean(centered * centered) + 1e-12)
        return centered * scale, scale

    def norm_back(grad, normal, scale):
        return scale * (grad - mean(grad) - normal * mean(grad * normal))

    def column(value):
        return jnp.sum(value, axis=0, keepdims=True)

    normed_at = 2 * quarter
    mixed_at = normed_at + width
    branch_at = mixed_at + width
    act_at = 5 * quarter
    for (first, count), pieces in zip(groups, mixed_refs):
        size = count * head_dim
        for at in range(ZS):
            low = mixed_at + (z_at ^ at) * part + first * head_dim
            send_ref[pl.ds(pl.multiple_of(low, head_dim), size), :] = pieces[at][...]
    mixed = send_ref[mixed_at:branch_at, :].T
    for copy in copies[0]:
        copy.wait()
    first_n, first_r = norm(tokens_ref[...] + (matmul(mixed, out_w[...]) + vec_ref[2:3, :]))
    normed = first_n * vec_ref[3:4, :] + vec_ref[4:5, :]
    low = normed.astype(BF16)
    send_ref[normed_at:mixed_at, :] = low.T
    for copy in copies[1] + copies[2]:
        copy.wait()
    quarters = []
    for half in range(2):
        for kept in (False, True):
            at = half * 2 * quarter + (core if kept else 1 - core) * quarter
            quarters.append((half, kept, pl.multiple_of(at, quarter)))
    acc = None
    for at, (half, kept, start) in enumerate(quarters):
        cut = pl.ds(start, quarter)
        pre_act = matmul(low, up_w[:, cut]) + upoff_ref[:, cut]
        phi = 0.5 + 0.5 * lax.erf(pre_act * (0.5**0.5))
        act = (pre_act * phi).astype(BF16)
        slope_ref[:, at * quarter : (at + 1) * quarter] = phi + pre_act * (
            jnp.exp(-0.5 * pre_act * pre_act) * 0.3989422804014327
        )
        target, base = (keep_ref, 0) if kept else (send_ref, act_at)
        target[base + half * quarter : base + (half + 1) * quarter, :] = act.T
        term = matmul(act, down_w[cut, :])
        acc = term if acc is None else acc + term
    second_n, second_r = norm(normed + (acc + vec_ref[5:6, :]))
    outputs_ref[...] = second_n * vec_ref[6:7, :] + vec_ref[7:8, :]
    place = lax.broadcasted_iota(jnp.int32, (rows, 1), 0)
    seed = jnp.where(place < meta_ref[0], seed_ref[...], 0.0)
    sum_grad = norm_back(seed * vec_ref[6:7, :], second_n, second_r)
    ffn = sum_grad.astype(BF16)
    for at in range(width // 256):
        low_row = act_at + 2 * quarter + at * rows
        send_ref[low_row : low_row + rows, :] = ffn[:, at * 256 : (at + 1) * 256]
    small_ref[3:4, :] = column(ffn.astype(F32))
    small_ref[4:5, :] = column(seed * second_n)
    small_ref[5:6, :] = column(seed)
    acc = sum_grad
    for at, (half, kept, start) in enumerate(quarters):
        cut = pl.ds(start, quarter)
        pre = right_trans(ffn, down_w[cut, :]) * slope_ref[:, at * quarter : (at + 1) * quarter]
        pre = pre.astype(BF16)
        target, base = (keep_ref, 2 * quarter) if kept else (send_ref, 0)
        for block in range(quarter // 256):
            row = base + (half * (quarter // 256) + block) * rows
            target[row : row + rows, :] = pre[:, block * 256 : (block + 1) * 256]
        sums = column(pre.astype(F32))
        line = 8 + half * (2 * quarter // width) + (core if kept else 1 - core)
        small_ref[pl.ds(line, 1), :] = sums
        acc = acc + right_trans(pre, up_w[:, cut])
    small_ref[1:2, :] = column(acc * first_n)
    small_ref[2:3, :] = column(acc)
    resid = norm_back(acc * vec_ref[3:4, :], first_n, first_r)
    resid_ref[...] = resid
    branch = resid.astype(BF16)
    wide_ref[...] = branch
    side = width // 2
    for target, base, which in (
        (send_ref, branch_at, 1 - core),
        (keep_ref, 4 * quarter, core),
    ):
        values = wide_ref[:, pl.ds(pl.multiple_of(which * side, 128), side)]
        target[base : base + rows, :] = values[:, :256]
        target[base + rows : base + 2 * rows, : side - 256] = values[:, 256:]
        target[base + rows : base + 2 * rows, side - 256 :] = jnp.zeros(
            (rows, 512 - side), BF16
        )
    small_ref[0:1, :] = column(branch.astype(F32))
    small_ref[6:8, :] = jnp.zeros((2, width), F32)
    small_ref[12:16, :] = jnp.zeros((4, width), F32)
    gap = branch_at + 2 * rows
    send_ref[gap:act_at, :] = jnp.zeros((act_at - gap, 256), BF16)
    tall_ref[...] = right_trans(out_w[...], branch).astype(BF16)
    for at in range(ZS):
        start = pl.multiple_of((z_at ^ at) * part, part)
        mgrad_refs[at][...] = tall_ref[pl.ds(start, part), :]


def middle(meta, mixed, groups, tokens, seed, vec, upoff, weights):
    rows, width = tokens.shape
    hidden = upoff.shape[1]
    in_vmem = pl.BlockSpec(memory_space=pltpu.VMEM)
    in_place = pl.BlockSpec(memory_space=pl.ANY)
    flat = [item for group in mixed for item in group]
    part = jax.ShapeDtypeStruct((width // ZS, rows), BF16)
    return pl.pallas_call(
        partial(middle_kernel, groups=groups, shared=len(weights) == 5),
        grid_spec=pltpu.PrefetchScalarGridSpec(
            num_scalar_prefetch=1,
            grid=(),
            in_specs=[in_vmem] * (4 + len(flat)) + [in_place] * len(weights),
            out_specs=[in_vmem] * (5 + ZS),
            scratch_shapes=[
                pltpu.VMEM((width, width), BF16),
                pltpu.VMEM((width, hidden), BF16),
                pltpu.VMEM((hidden, width), BF16),
                pltpu.VMEM((rows, hidden), F32),
                pltpu.VMEM((rows, width), BF16),
                pltpu.VMEM((width, rows), BF16),
                pltpu.SemaphoreType.DMA((11,)),
            ],
        ),
        out_shape=[jax.ShapeDtypeStruct((rows, width), F32)] * 2
        + [part] * ZS
        + [
            jax.ShapeDtypeStruct((2 * hidden, 256), BF16),
            jax.ShapeDtypeStruct((hidden + 2 * rows, 256), BF16),
            jax.ShapeDtypeStruct((16, width), F32),
        ],
        compiler_params=pltpu.CompilerParams(vmem_limit_bytes=VMEM_LIMIT),
        cost_estimate=work(15),
        name="middle",
    )(meta, tokens, seed, vec, upoff, *flat, *weights)


def down_kernel(meta_ref, keep_ref, got_ref, own_ffn_ref, got_ffn_ref, out_ref):
    keep, got = keep_ref[...], got_ref[...]
    rows = keep.shape[1]
    for at in range(out_ref.shape[1] // 256):
        cut = slice(at * rows, (at + 1) * rows)
        value = matmul(keep, own_ffn_ref[cut, :]) + matmul(got, got_ffn_ref[cut, :])
        out_ref[:, at * 256 : (at + 1) * 256] = value.astype(BF16)


def down_slab(meta, keep, send, got):
    block = send.shape[0] // 8
    kept = pl.BlockSpec((block, send.shape[1]), lambda i, m: (m[0], 0))
    act = pl.BlockSpec((block, send.shape[1]), lambda i, m: (5 + m[0], 0))
    ffn = pl.BlockSpec((block, send.shape[1]), lambda i, m: (7, 0))
    return pl.pallas_call(
        down_kernel,
        grid_spec=pltpu.PrefetchScalarGridSpec(
            num_scalar_prefetch=1,
            grid=(1,),
            in_specs=[kept, act, ffn, ffn],
            out_specs=pl.BlockSpec((block, block), lambda i, m: (0, 0)),
        ),
        out_shape=jax.ShapeDtypeStruct((block, block), BF16),
        compiler_params=pltpu.CompilerParams(vmem_limit_bytes=24 << 20),
        cost_estimate=work(2),
        name="down_slab",
    )(meta, keep, got, send, got)


def up_kernel(meta_ref, keep_ref, send_ref, got_ref, own_small_ref, got_small_ref, *refs):
    out_refs, table_ref = refs[:2], refs[2]
    rows = send_ref.shape[1]
    width = own_small_ref.shape[1]
    block = width // 4
    side = width // 2
    normed_at = 2 * width
    branch_at = normed_at + 2 * width
    x_at = meta_ref[0]
    pre_keep = 2 * width
    for w in range(2):
        small = own_small_ref[...] + got_small_ref[...]
        table_ref[...] = jnp.zeros_like(table_ref)
        for at in range(side // 128):
            low = w * side + at * 128
            table_ref[at * 8 : (at + 1) * 8, :] = small[:8, low : low + 128]
        base = side // 128 * 8
        for at in range(2 * width // 128):
            line = 8 + 2 * w + at // (width // 128)
            low = at % (width // 128) * 128
            table_ref[base + at : base + at + 1, :] = small[line : line + 1, low : low + 128]
        for out_ref, which in zip(out_refs, (1 - x_at, x_at)):
            start = pl.multiple_of(which * block, block)
            target = slice(w * block, (w + 1) * block)
            own = send_ref[pl.ds(normed_at + w * side + start, block), :]
            got = got_ref[pl.ds(normed_at + w * side + start, block), :]
            for at in range(normed_at // rows):
                cut = slice(at * rows, (at + 1) * rows)
                value = matmul(own, keep_ref[pre_keep + at * rows : pre_keep + (at + 1) * rows, :])
                value = value + matmul(got, got_ref[cut, :])
                out_ref[target, at * 256 : (at + 1) * 256] = value.astype(BF16)
            own = send_ref[pl.ds(normed_at + width + w * side + start, block), :]
            got = got_ref[pl.ds(normed_at + width + w * side + start, block), :]
            lane = normed_at // rows * 256
            for at in range(2):
                mine = 4 * width + at * rows
                theirs = branch_at + at * rows
                value = matmul(own, keep_ref[mine : mine + rows, :])
                value = value + matmul(got, got_ref[theirs : theirs + rows, :])
                value = value[:, : min(256, side - at * 256)].astype(BF16)
                out_ref[target, lane : lane + value.shape[1]] = value
                lane += value.shape[1]
            out_ref[target, lane : lane + 128] = table_ref[pl.ds(start, block), :].astype(BF16)


def up_slabs(meta, keep, send, got, own_small, got_small):
    width = own_small.shape[1]
    columns = 2 * width + width // 2 + 128
    first = pl.BlockSpec((5 * width, send.shape[1]), lambda i, m: (0, 0))

    def whole(value):
        return pl.BlockSpec(value.shape, lambda i, m: (0, 0))

    return pl.pallas_call(
        up_kernel,
        grid_spec=pltpu.PrefetchScalarGridSpec(
            num_scalar_prefetch=1,
            grid=(1,),
            in_specs=[whole(keep), first, first, whole(own_small), whole(own_small)],
            out_specs=[pl.BlockSpec((width // 2, columns), lambda i, m: (0, 0))] * 2,
            scratch_shapes=[pltpu.VMEM((width // 2, 128), F32)],
        ),
        out_shape=[jax.ShapeDtypeStruct((width // 2, columns), BF16)] * 2,
        compiler_params=pltpu.CompilerParams(vmem_limit_bytes=40 << 20),
        cost_estimate=work(4),
        name="up_slabs",
    )(meta, keep, send, got, own_small, got_small)


def key_sum_kernel(own_ref, core_ref, got_ref, *out_refs):
    size = out_refs[0].shape[1]
    for at, ref in enumerate(out_refs):
        cut = slice(at * size, (at + 1) * size)
        kept = (own_ref[cut, :].astype(F32) + core_ref[cut, :].astype(F32)).astype(BF16)
        ref[...] = (kept.astype(F32) + got_ref[cut, :].astype(F32)).astype(BF16).T


def key_sum(own, core, got):
    rows, columns = got.shape
    half = pl.BlockSpec((rows, columns), lambda i: (0, 0))
    return pl.pallas_call(
        key_sum_kernel,
        grid=(1,),
        in_specs=[half] * 3,
        out_specs=[pl.BlockSpec((columns, rows // ZS), lambda i: (0, 0))] * ZS,
        out_shape=[jax.ShapeDtypeStruct((columns, rows // ZS), BF16)] * ZS,
        compiler_params=pltpu.CompilerParams(vmem_limit_bytes=24 << 20),
        cost_estimate=work(2),
        name="key_sum",
    )(own, core, got)


def head_kernel(meta_ref, *refs):
    turned_refs, query_refs, kv_refs = refs[:2], refs[2 : 2 + ZS], refs[2 + ZS : 2 + 2 * ZS]
    refs = refs[2 + 2 * ZS :]
    out_ref = refs[-1]
    block = turned_refs[0].shape[0]

    def put(value, rows):
        columns = value.shape[1]
        if len(refs) == 2:
            value = value + refs[0][rows, :columns].astype(F32)
        out_ref[rows, :columns] = value.astype(BF16)
        out_ref[rows, columns:] = jnp.zeros((value.shape[0], out_ref.shape[1] - columns), BF16)

    grads = [jnp.concatenate([ref[...] for ref in items], axis=1) for items in (query_refs, kv_refs)]
    grads = jnp.concatenate(grads, axis=0)
    turned = jnp.concatenate([ref[...] for ref in turned_refs], axis=1)
    put(right_trans(turned, grads), slice(0, block))
    ones = jnp.ones((16, turned.shape[1]), BF16)
    put(right_trans(ones, grads), slice(block, block + 16))


def head_slab(meta, turned, query, kv, count, slabs, got=None, first=0):
    width, rows = turned[0].shape
    block = width // count
    columns = -(-(query[0].shape[0] + kv[0].shape[0]) // 128) * 128
    return pl.pallas_call(
        head_kernel,
        grid_spec=pltpu.PrefetchScalarGridSpec(
            num_scalar_prefetch=1,
            grid=(slabs,),
            in_specs=[pl.BlockSpec((block, rows), lambda i, m: (m[i] * 2 + m[slabs], 0))] * 2
            + [pl.BlockSpec(item.shape, lambda i, m: (0, 0)) for item in [*query, *kv]]
            + (
                []
                if got is None
                else [pl.BlockSpec((block + 16, columns), lambda i, m: (first + i, 0))]
            ),
            out_specs=pl.BlockSpec((block + 16, columns), lambda i, m: (i, 0)),
        ),
        out_shape=jax.ShapeDtypeStruct((slabs * (block + 16), columns), BF16),
        compiler_params=pltpu.CompilerParams(vmem_limit_bytes=24 << 20),
        cost_estimate=work(2),
        name="head_slab",
    )(meta, *turned, *query, *kv, *(() if got is None else (got,)))


def token_kernel(meta_ref, resid_ref, *refs, shared):
    query_refs, kv_refs, refs = refs[:ZS], refs[ZS : 2 * ZS], refs[2 * ZS :]
    weight_refs, refs = refs[: 5 if shared else 3], refs[5 if shared else 3 :]
    out_ref, full_ref, turned_ref, sems = refs
    w_at, c_at, z_at = meta_ref[1], meta_ref[2], meta_ref[3]
    width = full_ref.shape[1]
    moves = []
    if shared:
        count = weight_refs[0].shape[0]
        half = count // 2
        for kind in range(3):
            start = pl.multiple_of(w_at * count, count)
            moves.append((weight_refs[kind], full_ref.at[kind, pl.ds(start, count), :]))
            for ref, core in ((weight_refs[3], c_at), (weight_refs[4], 1 - c_at)):
                start = pl.multiple_of(((1 - w_at) * 2 + core) * half, half)
                moves.append(
                    (
                        ref.at[pl.ds(kind * half, half), :],
                        full_ref.at[kind, pl.ds(start, half), :],
                    )
                )
    else:
        for kind in range(3):
            moves.append((weight_refs[kind], full_ref.at[kind]))
    copies = []
    for at, (source, target) in enumerate(moves):
        copies.append(pltpu.make_async_copy(source, target, sems.at[at]))
        copies[-1].start()
    part = width // ZS
    head_dim = width // HEADS
    for at in range(ZS):
        low = (z_at ^ at) * part
        turned_ref[0, pl.ds(pl.multiple_of(low, part), part), :] = query_refs[at][...]
        for head in range(part // head_dim):
            start = pl.ds(pl.multiple_of(low + head * head_dim, head_dim), head_dim)
            for kind in (1, 2):
                row = (2 * head + kind - 1) * head_dim
                turned_ref[kind, start, :] = kv_refs[at][row : row + head_dim, :]
    parts = [turned_ref[kind].T for kind in range(3)]
    for copy in copies:
        copy.wait()
    out = resid_ref[...]
    for kind in range(3):
        out = out + right_trans(parts[kind], full_ref[kind])
    out_ref[...] = out


def token_gradient(meta, resid, query, kv, weights):
    rows, width = resid.shape
    in_vmem = pl.BlockSpec(memory_space=pltpu.VMEM)
    in_place = pl.BlockSpec(memory_space=pl.ANY)
    return pl.pallas_call(
        partial(token_kernel, shared=len(weights) == 5),
        grid_spec=pltpu.PrefetchScalarGridSpec(
            num_scalar_prefetch=1,
            grid=(),
            in_specs=[in_vmem] * (1 + 2 * ZS) + [in_place] * len(weights),
            out_specs=in_vmem,
            scratch_shapes=[
                pltpu.VMEM((3, width, width), BF16),
                pltpu.VMEM((3, width, rows), BF16),
                pltpu.SemaphoreType.DMA((9,)),
            ],
        ),
        out_shape=jax.ShapeDtypeStruct((rows, width), F32),
        compiler_params=pltpu.CompilerParams(vmem_limit_bytes=32 << 20),
        cost_estimate=work(4),
        name="token_gradient",
    )(meta, resid, *query, *kv, *weights)


def down_finish_kernel(meta_ref, *refs):
    block = refs[0].shape[0] // 4
    c_at, x_at = meta_ref[0], meta_ref[1]
    for at in range(4):
        for z in range(4):
            place = (c_at ^ (at >> 1)) * 8 + z * 2 + (x_at ^ (at & 1))
            start = pl.multiple_of(place * block, 8)
            refs[4][pl.ds(start, block), :] = refs[at][z * block : (z + 1) * block, :].astype(F32)


def down_finish(meta, pieces):
    block, width = pieces[0].shape
    in_vmem = pl.BlockSpec(memory_space=pltpu.VMEM)
    return pl.pallas_call(
        down_finish_kernel,
        grid_spec=pltpu.PrefetchScalarGridSpec(
            num_scalar_prefetch=1, grid=(), in_specs=[in_vmem] * 4, out_specs=in_vmem
        ),
        out_shape=jax.ShapeDtypeStruct((4 * block, width), F32),
        compiler_params=pltpu.CompilerParams(vmem_limit_bytes=32 << 20),
        cost_estimate=work(4),
        name="down_finish",
    )(meta, *pieces)


def up_finish_kernel(meta_ref, *refs):
    pieces = refs[:4]
    up_ref, out_ref, small_ref = refs[4:]
    block = pieces[0].shape[0]
    quarter = up_ref.shape[1] // 4
    side = out_ref.shape[1] // 2
    c_at, x_at = meta_ref[0], meta_ref[1]
    for at in range(4):
        start = pl.multiple_of((x_at ^ (at & 1)) * block, 8)
        rows = pl.ds(start, block)
        core = c_at ^ (at >> 1)
        for half in range(2):
            lanes = pl.ds(pl.multiple_of((2 * half + core) * quarter, 128), quarter)
            up_ref[rows, lanes] = pieces[at][:, half * quarter : (half + 1) * quarter].astype(F32)
        out_ref[rows, pl.ds(pl.multiple_of(core * side, 128), side)] = (
            pieces[at][:, 2 * quarter : 2 * quarter + side].astype(F32)
        )
        if at < 2:
            small_ref[rows, :] = pieces[at][:, 2 * quarter + side :].astype(F32)


def up_finish(meta, pieces, hidden, width):
    block = pieces[0].shape[0]
    in_vmem = pl.BlockSpec(memory_space=pltpu.VMEM)
    shapes = [(2 * block, hidden), (2 * block, width), (2 * block, 128)]
    return pl.pallas_call(
        up_finish_kernel,
        grid_spec=pltpu.PrefetchScalarGridSpec(
            num_scalar_prefetch=1,
            grid=(),
            in_specs=[in_vmem] * 4,
            out_specs=[in_vmem] * 3,
        ),
        out_shape=[jax.ShapeDtypeStruct(shape, F32) for shape in shapes],
        compiler_params=pltpu.CompilerParams(vmem_limit_bytes=40 << 20),
        cost_estimate=work(5),
        name="up_finish",
    )(meta, *pieces)


def head_finish_kernel(meta_ref, own_ref, got_ref, query_ref, key_ref, value_ref, bias_ref, *, part):
    size = own_ref.shape[0] // ZS
    block = size - 16
    head_dim = part // 3
    for at, source in enumerate((own_ref, got_ref)):
        start = pl.multiple_of((meta_ref[0] ^ at) * block, 8)
        rows = pl.ds(start, block)
        keys, values, queries = [], [], []
        for z in range(ZS):
            item = source[((z & 1) * 2 + (z >> 1)) * size :][:size].astype(F32)
            for head in range(3):
                low = part + head * 2 * head_dim
                keys.append(item[:, low : low + head_dim])
                values.append(item[:, low + head_dim : low + 2 * head_dim])
            queries.append(item[:, :part])
        key = jnp.concatenate(keys, axis=1)
        value = jnp.concatenate(values, axis=1)
        query = jnp.concatenate(queries, axis=1)
        query_ref[rows, :] = query[:block]
        key_ref[rows, :] = key[:block]
        value_ref[rows, :] = value[:block]
        if at == 0:
            bias_ref[0:8, :] = query[block : block + 8]
            bias_ref[8:16, :] = value[block : block + 8]


def head_finish(meta, own, got, width):
    rows = own.shape[0]
    rows = 2 * (rows // ZS - 16)
    return small_call(
        partial(head_finish_kernel, part=width // ZS),
        meta,
        (own, got),
        [((rows, width), F32)] * 3 + [((16, width), F32)],
        limit=40,
        name="head_finish",
    )


def in_order(index, own, other, axis):
    return jnp.where(
        index == 0,
        jnp.concatenate([own, other], axis=axis),
        jnp.concatenate([other, own], axis=axis),
    )


def part_of(value, index, count, axis):
    size = value.shape[axis] // count
    return lax.dynamic_slice_in_dim(value, index * size, size, axis)


def body(
    inputs,
    lengths,
    cotangent,
    query_weight,
    query_bias,
    key_weight,
    value_weight,
    value_bias,
    output_weight,
    output_bias,
    first_gain,
    first_shift,
    up_weight,
    up_bias,
    down_weight,
    down_bias,
    second_gain,
    second_shift,
    *,
    sizes,
):
    count_o, count_w = sizes
    w_at = lax.axis_index("w")
    z_at = lax.axis_index("z")
    c_at = lax.axis_index("c")
    x_at = lax.axis_index("x")
    o_at = lax.axis_index("o")
    tokens = inputs[0]
    local_rows, width = tokens.shape
    head_dim = width // HEADS
    heads = HEADS // ZS
    part = heads * head_dim
    length = lengths[0]

    hold = lax.optimization_barrier

    near = ((0, 1), (1, 0), (2, 3), (3, 2))
    far = ((0, 2), (2, 0), (1, 3), (3, 1))
    cross = ((0, 3), (3, 0), (1, 2), (2, 1))

    def exchange(pieces):
        return [pieces[0]] + [
            lax.ppermute(item, "z", perm) for item, perm in zip(pieces[1:], (near, far, cross))
        ]

    own_rows = query_weight.shape[0]
    big_weights = (output_weight, up_weight, down_weight)
    sides = jnp.stack([z_at, c_at]).astype(jnp.int32)
    low_tokens = tokens.astype(BF16)
    kv_own, query_own, *low_heads, head_pack = prepare(
        sides, (query_weight, key_weight, value_weight)
    )
    line_tokens = [low_tokens, lax.ppermute(low_tokens, "z", near)]
    line_tokens.append(lax.ppermute(low_tokens, "z", far))
    early = jnp.stack([query_bias, value_bias]).astype(BF16)
    late = jnp.stack(
        [
            item.reshape(-1, own_rows)[row]
            for item in (
                output_bias,
                first_gain,
                first_shift,
                down_bias,
                second_gain,
                second_shift,
                up_bias,
            )
            for row in range(item.shape[0] // own_rows)
        ]
    )
    if count_w == 2:
        kv_other, query_other, early_got = [
            swap(item, "w") for item in (kv_own, query_own, early)
        ]
        *low_weights, weight_pack = round_weights(sides, big_weights)
        kv_other, query_other, early_got, weight_pack, *line_tokens[1:3] = hold(
            (kv_other, query_other, early_got, weight_pack, *line_tokens[1:3])
        )
        weight_got = swap(weight_pack, "w")
        sources = (kv_own, query_own, kv_other, query_other, early, early_got)
    else:
        attn_own = jnp.concatenate([kv_own, query_own], axis=1)
        attn_full = lax.all_gather(attn_own, "w", axis=0, tiled=True)
        small = jnp.concatenate([early, late.astype(BF16)], axis=0)
        small_all = lax.all_gather(small, "w", axis=0, tiled=False)
        low_weights = [item.astype(BF16) for item in big_weights]
        weight_got = [lax.all_gather(item, "w", axis=0, tiled=True) for item in low_weights]
        head_weights = [lax.all_gather(item, "w", axis=0, tiled=True) for item in low_heads]
        pair = jnp.transpose(small_all[:, :2], (1, 0, 2)).reshape(2, width).astype(F32)
        own_bias = lax.dynamic_slice_in_dim(pair, z_at * part, part, 1)
        value_bias_own = own_bias[1].reshape(heads, 1, head_dim)
        kv_bias = jnp.concatenate([jnp.zeros_like(value_bias_own), value_bias_own], axis=1)
        bias_row = jnp.concatenate([kv_bias.reshape(1, 2 * part), own_bias[:1]], axis=1)
        sources = (attn_full, bias_row)

    line_tokens.append(lax.ppermute(line_tokens[2], "z", near))
    corner = jnp.stack([w_at, z_at]).astype(jnp.int32)
    made = [project(corner, *line_tokens[:2], sources)]
    made[0], *line_tokens[2:] = hold((made[0], *line_tokens[2:]))
    made.append(project(corner, *line_tokens[2:], sources))
    queries = [item[0] for item in made]
    turned = [item[2] for item in made]
    kv_blocks = [[item[1] for item in made]]
    for axis in ("x", "c", "o")[: 3 if count_o == 2 else 2]:
        kv_blocks = kv_blocks + [[swap(item, axis) for item in pair] for pair in kv_blocks]
    places = []
    for at in range(4 * count_o):
        o_of = o_at ^ (at >> 2)
        places.append(o_of * 16 + (x_at ^ (at & 1)) * 2 + (c_at ^ ((at >> 1) & 1)))
    meta = jnp.stack([length, z_at] + places).astype(jnp.int32)
    kv_blocks = [
        [pltpu.with_memory_space_constraint(item, pltpu.MemorySpace.HBM) for item in pair]
        for pair in kv_blocks
    ]
    attended, *made = attend_forward(meta, queries, kv_blocks, heads)
    logs = made[ZS]
    if count_w == 2:
        attended, weight_got, head_pack, late = hold((attended, weight_got, head_pack, late))
        late = late.astype(BF16)
        small_own = jnp.concatenate([early, late], axis=0)
        small_got = jnp.concatenate([early_got, swap(late, "w")], axis=0)
        small_all = in_order(w_at, small_own[None], small_got[None], 0)
        weights = [*low_weights, weight_got, swap(weight_got, "c")]
        head_got = swap(head_pack, "w")
    else:
        weights = weight_got
    mixed = exchange(made[:ZS])
    small_all = small_all.astype(F32)
    vec = jnp.transpose(small_all[:, :8], (1, 0, 2)).reshape(8, width)
    up_offset = small_all[:, 8:].reshape(1, -1)

    split = count_w == 2 and count_o == 1
    my_index = o_at * 16 + z_at * 4 + x_at * 2 + c_at
    rest = jnp.clip(length - my_index * local_rows, 0, local_rows)
    core = c_at if split else jnp.zeros_like(c_at)
    spots = jnp.stack([rest, w_at, core, z_at]).astype(jnp.int32)
    outputs, resid_grad, *made = middle(
        spots, [mixed], ((0, heads),), tokens, cotangent[0], vec, up_offset, weights
    )
    head_grads = exchange(made[:ZS])
    send, keep, small_own = made[ZS:]
    hidden = up_offset.shape[1]

    near_bit, far_bit = z_at & 1, z_at >> 1

    def add_pair(kept, got):
        return (kept.astype(F32) + got.astype(F32)).astype(BF16)

    def join(value, got, bit):
        return in_order(bit, value, got, 0)

    spot = jnp.stack([c_at, x_at]).astype(jnp.int32)
    token = [spot]

    def arrive(*values):
        token[0], *values = hold((token[0], *values))
        return values[0] if len(values) == 1 else values

    def backward(first, count, made=()):
        return attend_backward(
            meta, queries, head_grads, attended, logs, kv_blocks, first, count, made
        )

    def to_near(value):
        return lax.ppermute(value, "z", near)

    def to_far(value):
        return lax.ppermute(value, "z", far)

    def head_part(ws, core, got=None, first=0):
        at = jnp.stack([jnp.asarray(item) for item in (*ws, core)]).astype(jnp.int32)
        return head_slab(at, turned, query_low, kv_low, 2 * count_w, len(ws), got, first)

    def pick(w, c):
        return jnp.stack([jnp.asarray(w), jnp.asarray(c)]).astype(jnp.int32)

    if split:
        got, small_got = swap(send, "c"), swap(small_own, "c")
        down_far = down_slab(pick(1 - w_at, 0), keep, send, got)
        up_sent, up_kept = up_slabs(
            jnp.stack([x_at]).astype(jnp.int32), keep, send, got, small_own, small_got
        )
        down_near = down_slab(pick(1 * w_at, 0), keep, send, got)
        down_far, up_sent, down_near, *head_grads = hold(
            (down_far, up_sent, down_near, *head_grads)
        )
        made = backward(0, heads - 1)
        down_got, *made = arrive(swap(down_far, "w"), *made)
        down_sum = add_pair(down_near, down_got)
        down_got = to_near(part_of(down_sum, 1 - near_bit, 2, 0))
        down_sum, *head_grads = arrive(down_sum, *head_grads)
        made = backward(heads - 1, 1, made)
        down_got, up_got, head_got, *made = arrive(
            down_got, swap(up_sent, "x"), head_got, *made
        )
        query_low, pairs = made[:ZS], made[ZS:]
        head_weights = [*low_heads, head_got, swap(head_got, "c")]
        pair_got = swap(pairs[1], "c")
        query_got = exchange(query_low)
        down_sum = add_pair(part_of(down_sum, near_bit, 2, 0), down_got)
        down_got = to_far(part_of(down_sum, 1 - far_bit, 2, 0))
        up_sum = add_pair(up_kept, up_got).reshape(2, own_rows // 2, -1)
        up_got = swap(lax.dynamic_index_in_dim(up_sum, 1 - w_at, 0, keepdims=False), "w")
        pair_got = arrive(pair_got)
        half_rows = pair_got.shape[0] // 2
        pair_sent = add_pair(pairs[0][half_rows:], pair_got[half_rows:])
        pair_sent = arrive(pair_sent)
        key_got = swap(pair_sent, "x")
        key_got, down_got, up_got, *query_got = arrive(key_got, down_got, up_got, *query_got)
        up_sum = add_pair(lax.dynamic_index_in_dim(up_sum, w_at, 0, keepdims=False), up_got)
        up_sent, key_got = arrive(part_of(up_sum, 1 - near_bit, 2, 0), key_got)
        up_got = to_near(up_sent)
        kv_low = key_sum(pairs[0], pair_got, key_got)
        down_sum = add_pair(part_of(down_sum, far_bit, 2, 0), down_got)
        down_got = swap(part_of(down_sum, 1 - x_at, 2, 0), "x")
        head_core = swap(head_part((1 - w_at, 1 * w_at), 1 - c_at), "c")
        kv_got = exchange(kv_low)
        down_got = arrive(down_got)
        down_sum = add_pair(part_of(down_sum, x_at, 2, 0), down_got)
        down_got = to_far(down_sum)
        head_core = arrive(head_core)
        head_sent = swap(head_part((1 - w_at,), c_at, head_core), "w")
        head_sum = head_part((1 * w_at,), c_at, head_core, 1)
        up_got = arrive(up_got)
        up_sum = add_pair(part_of(up_sum, near_bit, 2, 0), up_got)
        up_got = to_far(part_of(up_sum, 1 - far_bit, 2, 0))
        head_sent = arrive(head_sent)
        head_sum = add_pair(head_sum, head_sent)
        head_got = swap(head_sum, "x")
        kv_got = arrive(*kv_got)
        input_grad = token_gradient(
            spots, resid_grad, query_got, kv_got, head_weights
        )
        up_got = arrive(up_got)
        up_sum = add_pair(part_of(up_sum, far_bit, 2, 0), up_got)
        up_got = to_far(up_sum)
        down_got = arrive(down_got)
        down_sum = join(down_sum[None], down_got[None], far_bit)
        down_got = to_near(down_sum)
        head_got = arrive(head_got)
        head_sum = add_pair(head_sum, head_got)
        head_got = to_far(head_sum)
        up_got = arrive(up_got)
        up_sum = join(up_sum, up_got, far_bit)
        up_got = to_near(up_sum)
        down_got = arrive(down_got)
        down_sum = join(down_sum[None], down_got[None], near_bit)
        down_sum = down_sum.reshape(-1, width)
        down_x = swap(down_sum, "x")
        down_c = swap(down_sum, "c")
        head_got = arrive(head_got)
        head_two = join(head_sum, head_got, far_bit)
        head_got = to_near(head_two)
        up_got = arrive(up_got)
        up_sum = join(up_sum, up_got, near_bit)
        up_x = swap(up_sum, "x")
        up_c = swap(up_sum, "c")
        down_x, input_grad = arrive(down_x, input_grad)
        down_pieces = [down_sum, down_x, down_c, swap(down_x, "c")]
        head_got = arrive(head_got)
        head_four = join(head_two, head_got, near_bit)
        head_other = swap(head_four, "c")
        total_down = down_finish(spot, down_pieces)
        up_x, total_down = arrive(up_x, total_down)
        up_pieces = [up_sum, up_x, up_c, swap(up_x, "c")]
        total_query, total_key, total_value, head_bias = head_finish(
            spot, head_four, head_other, width
        )
        total_query, total_key, total_value = arrive(total_query, total_key, total_value)
        total_up, total_out, table = up_finish(token[0], up_pieces, hidden, width)
        groups = own_rows // 128
        small_total = table[: 8 * groups].reshape(groups, 8, 128)
        vectors = [small_total[:, at].reshape(own_rows) for at in range(6)]
        lines = hidden // count_w // 128
        total_up_bias = table[8 * groups : 8 * groups + lines].reshape(-1)
    else:
        made = backward(0, heads)
        query_low, pairs = made[:ZS], made[ZS:]
        if count_o == 2:
            pairs = [plus(spot, pairs[at], swap(pairs[at + 2], "o")) for at in range(2)]
        pair_got = swap(pairs[1], "c")
        half_rows = pair_got.shape[0] // 2
        key_got = swap(plus(spot, pairs[0], pair_got, half_rows), "x")
        kv_low = key_sum(pairs[0], pair_got, key_got)
        if count_w == 2:
            head_weights = [*low_heads, head_got, swap(head_got, "c")]
        input_grad = token_gradient(
            spots.at[2].set(c_at.astype(jnp.int32)),
            resid_grad,
            exchange(query_low),
            exchange(kv_low),
            head_weights,
        )
        every_w = tuple(range(count_w))
        slabs = head_part(every_w, c_at, swap(head_part(every_w, 1 - c_at), "c"))
        head_sum = lax.psum_scatter(slabs, "w", scatter_dimension=0, tiled=True)
        head_sum = plus(spot, head_sum, swap(head_sum, "x"))
        if count_o == 2:
            head_sum = plus(spot, head_sum, swap(head_sum, "o"))
        n_bit, f_bit = [
            jnp.stack([bit, bit]).astype(jnp.int32) for bit in (near_bit, far_bit)
        ]
        head_sum = unite(f_bit, head_sum, to_far(head_sum))
        head_sum = unite(n_bit, head_sum, to_near(head_sum))
        total_query, total_key, total_value, head_bias = head_finish(
            spot, head_sum, swap(head_sum, "c"), width
        )
        quarter = hidden // 4
        count = quarter // 256
        act_at = 5 * quarter
        act = [keep[:quarter], send[act_at : act_at + quarter], keep[quarter : 2 * quarter]]
        act += [send[act_at + quarter : act_at + 2 * quarter]]
        act = jnp.concatenate(act, axis=0)

        def rows_of(value, low, at):
            return value[low + at * local_rows : low + (at + 1) * local_rows]

        ffn_at = act_at + 2 * quarter
        ffn = jnp.concatenate([rows_of(send, ffn_at, at) for at in range(width // 256)], axis=1)
        pre = []
        for half in range(2):
            pre += [rows_of(keep, 2 * quarter, half * count + at) for at in range(count)]
            pre += [rows_of(send, 0, half * count + at) for at in range(count)]
        pre = jnp.concatenate(pre, axis=1)
        normed_turned = send[2 * quarter : 2 * quarter + width]
        mixed_turned = send[2 * quarter + width : 2 * quarter + 2 * width]
        side = width // 2
        branch = jnp.concatenate(
            [
                rows_of(keep, 4 * quarter, 0),
                rows_of(keep, 4 * quarter, 1)[:, : side - 256],
                rows_of(send, 2 * quarter + 2 * width, 0),
                rows_of(send, 2 * quarter + 2 * width, 1)[:, : side - 256],
            ],
            axis=1,
        )

        def sum_all(value):
            value = value.astype(BF16)
            value = lax.psum_scatter(value, "w", scatter_dimension=0, tiled=True)
            return lax.psum(value, ("o", "z", "x", "c")).astype(F32)

        total_down = sum_all(matmul(act, ffn))
        total_up = sum_all(matmul(normed_turned, pre))
        total_out = sum_all(matmul(mixed_turned, branch))
        small_own = lax.psum(small_own, ("o", "z", "x", "c", "w"))
        vectors = [part_of(small_own[at], w_at, count_w, 0) for at in range(6)]
        total_up_bias = part_of(small_own[8:12].reshape(-1), w_at, count_w, 0)

    totals = [part_of(head_bias[at], w_at, count_w, 0) for at in (0, 8)] + vectors
    return (
        outputs[None],
        input_grad[None],
        total_query,
        totals[0],
        total_key,
        total_value,
        totals[1],
        total_out,
        totals[2],
        totals[3],
        totals[4],
        total_up,
        total_up_bias,
        total_down,
        totals[5],
        totals[6],
        totals[7],
    )


def solution(mesh):
    count_s = mesh.shape["seq"]
    count_w = mesh.shape["wshard"]
    count_o = count_s // 16
    fine = Mesh(
        mesh.devices.reshape(count_o, ZS, 2, 2, count_w), ("o", "z", "x", "c", "w")
    )
    seq = ("o", "z", "x", "c")
    rows = P("w", seq, None)
    matrix = P("w", None)
    vector = P("w")
    placed = (
        rows,
        vector,
        rows,
        matrix,
        vector,
        matrix,
        matrix,
        vector,
        matrix,
        vector,
        vector,
        vector,
        matrix,
        vector,
        matrix,
        vector,
        vector,
        vector,
    )
    return jax.shard_map(
        partial(body, sizes=(count_o, count_w)),
        mesh=fine,
        in_specs=placed,
        out_specs=(
            rows,
            rows,
            matrix,
            vector,
            matrix,
            matrix,
            vector,
            matrix,
            vector,
            vector,
            vector,
            matrix,
            vector,
            matrix,
            vector,
            vector,
            vector,
        ),
        check_vma=False,
    )
```

profile of v0, /device:TPU:1, one launch (start us, length us, event | category | flops | bytes accessed | tf_op | source)
XLA Modules:
  0.0 319.3 jit_solution(17788954638541001761)
XLA Ops:
  6.9 4.6 %prepare.1 = (bf16[384,384]{1,0:T(8,128)(2,1)}, bf16[384,192]{1,0:T(8,128)(2,1)}, bf16[384,768]{1,0:T(8,128)(2,1)}, bf16[384,768]{1,0:T(8,128)(2,1)}, bf16[384,7...) custom-call(s32[2]{0:T(128)} %get-tuple-element.342.meta_ref, f32[384,768]{1,0:T(8,128)} %refs_0_.1, f32[384,768]{1,0:T(8,128)} %refs_1_.1, ...), custom_call_target="tpu_custom_call" | custom-call | flops 1000 | bytes 1 | tf_op jit(solution)/shard_map/prepare/pallas_call | solution.py:366
  14.5 8.3 %round_weights.1 = (bf16[384,768]{1,0:T(8,128)(2,1)}, bf16[384,3072]{1,0:T(8,128)(2,1)}, bf16[1536,768]{1,0:T(8,128)(2,1)}, bf16[1728,768]{1,0:T(8,128)(2,1)}) custom-call(s32[2]{0:T(128)} %get-tuple-element.342.meta_ref, f32[384,768]{1,0:T(8,128)} %out_w.1, f32[384,3072]{1,0:T(8,128)} %up_w.1, f32[1536,768]{1,0:T(8,128)} %down_w.1), custom_call_target="tpu_custom_call" | custom-call | flops 1000 | bytes 1 | tf_op jit(solution)/shard_map/round_weights/pallas_call | solution.py:264
  28.0 4.9 %collective-permute-done.5.second_ref = bf16[256,768]{1,0:T(8,128)(2,1)S(1)} collective-permute-done((bf16[256,768]{1,0:T(8,128)(2,1)S(1)}, bf16[256,768]{1,0:T(8,128)(2,1)S(1)}, u32[]{:S(2)}, u32[]{:S(2)}) %collective-permute-start.5) | collective-permute-done | bytes 393248 | tf_op jit(solution)/shard_map/ppermute | solution.py:1122
  37.5 3.8 %collective-permute-start.9 = (bf16[512,384]{1,0:T(8,128)(2,1)S(1)}, bf16[512,384]{1,0:T(8,128)(2,1)S(1)}, u32[]{:S(2)}, u32[]{:S(2)}) collective-permute-start(bf16[512,384]{1,0:T(8,128)(2,1)S(1)} %get-tuple-element.189.refs_3_.refs_9_), channel_id=1, source_target_pairs={{0,2},{2,0},{1,3},{3,1},{4,6},{6,4},{5,7},{7,5},{8,10},{10,8},{9,1... | collective-permute-start | bytes 1179656 | tf_op jit(solution)/shard_map/ppermute | solution.py:34
  43.5 7.9 %collective-permute-start.11 = (bf16[512,384]{1,0:T(8,128)(2,1)S(1)}, bf16[512,384]{1,0:T(8,128)(2,1)S(1)}, u32[]{:S(2)}, u32[]{:S(2)}) collective-permute-start(bf16[512,384]{1,0:T(8,128)(2,1)S(1)} %collective-permute-done.7.refs_5_.refs_11_), channel_id=1, source_target_pairs={{0,2},{2,0},{1,3},{3,1},{4,6},{6,4},{5,7},{7,5},{8,10},{10,8},{9,1... | collective-permute-start | bytes 1179656 | tf_op jit(solution)/shard_map/ppermute | solution.py:34
  51.9 4.1 %collective-permute-start.10 = (bf16[512,384]{1,0:T(8,128)(2,1)S(1)}, bf16[512,384]{1,0:T(8,128)(2,1)S(1)}, u32[]{:S(2)}, u32[]{:S(2)}) collective-permute-start(bf16[512,384]{1,0:T(8,128)(2,1)S(1)} %collective-permute-done.6.refs_4_.refs_10_), channel_id=1, source_target_pairs={{0,2},{2,0},{1,3},{3,1},{4,6},{6,4},{5,7},{7,5},{8,10},{10,8},{9,1... | collective-permute-start | bytes 1179656 | tf_op jit(solution)/shard_map/ppermute | solution.py:34
  58.7 25.9 %attend_forward.1 = (f32[192,1024]{1,0:T(8,128)}, bf16[192,256]{1,0:T(8,128)(2,1)}, bf16[192,256]{1,0:T(8,128)(2,1)}, bf16[192,256]{1,0:T(8,128)(2,1)}, bf16[192,256]{1,0:T(8,128)(2,1)}, /*index=5*/f32[3,1,1024]{2,1,0:T(1,128)}) custom-call(s32[6]{0:T(128)} %stack.103.meta_ref, bf16[192,512]{1,0:T(8,128)(2,1)} %copy-done.16, bf16[192,512]{1,0:T(8,128)(2,1)} %copy-done.17, ...), custom_call_target="tpu_custom_call" | custom-call | flops 24000 | bytes 1 | tf_op jit(solution)/shard_map/attend_forward/pallas_call | solution.py:125
  85.5 3.4 %collective-permute-start.16 = (bf16[192,256]{1,0:T(8,128)(2,1)}, bf16[192,256]{1,0:T(8,128)(2,1)S(1)}, u32[]{:S(2)}, u32[]{:S(2)}) collective-permute-start(bf16[192,256]{1,0:T(8,128)(2,1)} %get-tuple-element.197), channel_id=1, source_target_pairs={{0,24},{24,0},{8,16},{16,8},{1,25},{25,1},{9,17},{17,9},{2,26},{26... | collective-permute-start | bytes 294920 | tf_op jit(solution)/shard_map/ppermute | solution.py:1069
  89.1 2.3 collective-permute-done.13
  93.8 15.9 %middle.1 = (f32[256,768]{1,0:T(8,128)}, f32[256,768]{1,0:T(8,128)}, bf16[192,256]{1,0:T(8,128)(2,1)}, bf16[192,256]{1,0:T(8,128)(2,1)}, bf16[192,256]{1,0:T(8,1...) custom-call(s32[4]{0:T(128)} %pad_add_fusion.2.meta_ref, ...), custom_call_target="tpu_custom_call" | custom-call | flops 15000 | bytes 1 | tf_op jit(solution)/shard_map/middle/pallas_call | solution.py:641
  109.7 4.1 %collective-permute-start.18 = (bf16[6144,256]{1,0:T(8,128)(2,1)}, bf16[6144,256]{1,0:T(8,128)(2,1)S(1)}, u32[]{:S(2)}, u32[]{:S(2)}) collective-permute-start(bf16[6144,256]{1,0:T(8,128)(2,1)} %get-tuple-element.204.own_ffn_ref.send_ref), channel_id=1, source_target_pairs={{0,2},{2,0},{1,3},{3,1},{4,6},{6,4},{5,7},{7,5},{8,10},{10,8},{9,1... | collective-permute-start | bytes 9437192 | tf_op jit(solution)/shard_map/ppermute | solution.py:34
  125.0 2.3 down_slab.2
  127.9 2.9 up_slabs.1
  134.8 26.5 %attend_backward.2 = (bf16[192,256]{1,0:T(8,128)(2,1)}, bf16[192,256]{1,0:T(8,128)(2,1)}, bf16[192,256]{1,0:T(8,128)(2,1)}, bf16[192,256]{1,0:T(8,128)(2,1)}, bf...) custom-call(s32[6]{0:T(128)} %stack.103.meta_ref, bf16[192,512]{1,0:T(8,128)(2,1)} %copy-done.16, ...), custom_call_target="tpu_custom_call" | custom-call | flops 24000 | bytes 1 | tf_op jit(solution)/shard_map/attend_backward/pallas_call | solution.py:226
  165.3 14.6 %attend_backward.3 = (bf16[192,256]{1,0:T(8,128)(2,1)}, bf16[192,256]{1,0:T(8,128)(2,1)}, bf16[192,256]{1,0:T(8,128)(2,1)}, bf16[192,256]{1,0:T(8,128)(2,1)}, bf...) custom-call(s32[6]{0:T(128)} %stack.103.meta_ref, ...), custom_call_target="tpu_custom_call", output_to_operand_aliasing={{0}: (17, {}), {1}: (18, {}), {2}: (19, {}), {3}: (20, {}),... | custom-call | flops 12000 | bytes 1 | tf_op jit(solution)/shard_map/attend_backward/pallas_call | solution.py:226
  193.3 6.0 %collective-permute-done.31.refs_1_ = bf16[192,256]{1,0:T(8,128)(2,1)S(1)} collective-permute-done((bf16[192,256]{1,0:T(8,128)(2,1)S(1)}, bf16[192,256]{1,0:T(8,128)(2,1)S(1)}, u32[]{:S(2)}, u32[]{:S(2)}) %collective-permute-start.31) | collective-permute-done | bytes 98336 | tf_op jit(solution)/shard_map/ppermute | solution.py:1069
  201.6 11.3 %collective-permute-done.32.refs_2_ = bf16[192,256]{1,0:T(8,128)(2,1)S(1)} collective-permute-done((bf16[192,256]{1,0:T(8,128)(2,1)S(1)}, bf16[192,256]{1,0:T(8,128)(2,1)S(1)}, u32[]{:S(2)}, u32[]{:S(2)}) %collective-permute-start.32) | collective-permute-done | bytes 98336 | tf_op jit(solution)/shard_map/ppermute | solution.py:1069
  218.8 3.2 %head_slab.3 = bf16[416,640]{1,0:T(8,128)(2,1)} custom-call(s32[3]{0:T(128)S(1)} %pad_add_fusion.6.meta_ref, bf16[768,512]{1,0:T(8,128)(2,1)S(1)} %copy-done.6, bf16[768,512]{1,0:T(8,128)(2,1)S(1)} %copy-done.8, bf16[192,256]{1,0:T(8,128)(2,1)S(1)} %copy-done.15, bf16[192,256]{1,0:T(8,128)(2,1)S(1)} %copy-done.24, bf16[192,256]{1,0:T(8,128)(2,1)S(1)} %copy-done.26, ...), custom_call_target="tpu_custom_call" | custom-call | flops 2000 | bytes 1 | tf_op jit(solution)/shard_map/head_slab/pallas_call | solution.py:817
  235.5 7.5 %collective-permute-done.36 = bf16[96,2048]{1,0:T(8,128)(2,1)} collective-permute-done((bf16[96,2048]{1,0:T(8,128)(2,1)}, bf16[96,2048]{1,0:T(8,128)(2,1)}, u32[]{:S(2)}, u32[]{:S(2)}) %collective-permute-start.36) | collective-permute-done | bytes 393248 | tf_op jit(solution)/shard_map/ppermute | solution.py:1191
  245.7 3.9 %collective-permute-done.37 = bf16[208,640]{1,0:T(8,128)(2,1)S(1)} collective-permute-done((bf16[208,640]{1,0:T(8,128)(2,1)S(1)}, bf16[208,640]{1,0:T(8,128)(2,1)S(1)}, u32[]{:S(2)}, u32[]{:S(2)}) %collective-permute-start.37) | collective-permute-done | bytes 266272 | tf_op jit(solution)/shard_map/ppermute | solution.py:34
  252.8 9.1 %collective-permute-done.41 = bf16[48,2048]{1,0:T(8,128)(2,1)S(1)} collective-permute-done((bf16[48,2048]{1,0:T(8,128)(2,1)S(1)}, bf16[48,2048]{1,0:T(8,128)(2,1)S(1)}, u32[]{:S(2)}, u32[]{:S(2)}) %collective-permute-start.41) | collective-permute-done | bytes 196640 | tf_op jit(solution)/shard_map/ppermute | solution.py:1194
  262.1 2.3 collective-permute-start.44
  264.7 7.4 %collective-permute-done.44 = bf16[48,2048]{1,0:T(8,128)(2,1)S(1)} collective-permute-done((bf16[48,2048]{1,0:T(8,128)(2,1)S(1)}, bf16[48,2048]{1,0:T(8,128)(2,1)S(1)}, u32[]{:S(2)}, u32[]{:S(2)}) %collective-permute-start.44) | collective-permute-done | bytes 196640 | tf_op jit(solution)/shard_map/ppermute | solution.py:1194
  272.2 3.4 %collective-permute-start.47 = (bf16[96,2048]{1,0:T(8,128)(2,1)S(1)}, bf16[96,2048]{1,0:T(8,128)(2,1)S(1)}, u32[]{:S(2)}, u32[]{:S(2)}) collective-permute-start(bf16[96,2048]{1,0:T(8,128)(2,1)S(1)} %maximum_select_fusion.4), channel_id=1, source_target_pairs={{0,8},{8,0},{16,24},{24,16},{1,9},{9,1},{17,25},{25,17},{2,10},{10... | collective-permute-start | bytes 1179656 | tf_op jit(solution)/shard_map/ppermute | solution.py:1191
  276.5 7.9 %collective-permute-done.46 = bf16[208,640]{1,0:T(8,128)(2,1)S(1)} collective-permute-done((bf16[208,640]{1,0:T(8,128)(2,1)S(1)}, bf16[208,640]{1,0:T(8,128)(2,1)S(1)}, u32[]{:S(2)}, u32[]{:S(2)}) %collective-permute-start.46) | collective-permute-done | bytes 266272 | tf_op jit(solution)/shard_map/ppermute | solution.py:1194
  284.7 2.8 collective-permute-done.47
  288.3 3.8 %token_gradient.1 = f32[256,768]{1,0:T(8,128)} custom-call(s32[4]{0:T(128)S(1)} %copy-done.48, f32[256,768]{1,0:T(8,128)S(1)} %copy-done.36, bf16[192,256]{1,0:T(8,128)(2,1)S(1)} %copy-done.15, bf16[192,256]{1,0:T(8,128)(2,1)S(1)} %copy-done.42, bf16[192,256]{1,0:T(8,128)(2,1)S(1)} %copy-done.44, bf16[192,256]{1,0:T(8,128)(2,1)S(1)} %copy-done.46, ...), custom_call_target="tpu_custom_call" | custom-call | flops 4000 | bytes 1 | tf_op jit(solution)/shard_map/token_gradient/pallas_call | solution.py:889
  292.1 4.6 %collective-permute-start.52 = (bf16[384,768]{1,0:T(8,128)(2,1)S(1)}, bf16[384,768]{1,0:T(8,128)(2,1)S(1)}, u32[]{:S(2)}, u32[]{:S(2)}) collective-permute-start(bf16[384,768]{1,0:T(8,128)(2,1)S(1)} %bitcast.48), channel_id=1, source_target_pairs={{0,2},{2,0},{1,3},{3,1},{4,6},{6,4},{5,7},{7,5},{8,10},{10,8},{9,1... | collective-permute-start | bytes 1769480 | tf_op jit(solution)/shard_map/ppermute | solution.py:34
  301.7 3.0 down_finish.1
  304.8 3.9 %collective-permute-start.56 = (bf16[192,2048]{1,0:T(8,128)(2,1)}, bf16[192,2048]{1,0:T(8,128)(2,1)}, u32[]{:S(2)}, u32[]{:S(2)}) collective-permute-start(bf16[192,2048]{1,0:T(8,128)(2,1)} %collective-permute-done.51.refs_1_), channel_id=1, source_target_pairs={{0,2},{2,0},{1,3},{3,1},{4,6},{6,4},{5,7},{7,5},{8,10},{10,8},{9,1... | collective-permute-start | bytes 2359304 | tf_op jit(solution)/shard_map/ppermute | solution.py:34
  308.6 2.7 head_finish.1
  312.6 5.1 %up_finish.1 = (f32[384,3072]{1,0:T(8,128)}, f32[384,768]{1,0:T(8,128)}, f32[384,128]{1,0:T(8,128)S(1)}) custom-call(s32[2]{0:T(128)S(1)} %pad_add_fusion.5.meta_ref, bf16[192,2048]{1,0:T(8,128)(2,1)S(1)} %maximum_select_fusion.1.refs_0_, bf16[192,2048]{1,0:T(8,128)(2,1)} %collective-permute-done.51.refs_1_, ...), custom_call_target="tpu_custom_call" | custom-call | flops 5000 | bytes 1 | tf_op jit(solution)/shard_map/up_finish/pallas_call | solution.py:959
  (321 shorter events, 97.0 us)
Async XLA Ops:
  1.8 21.5 %collective-permute-start.3 = (bf16[256,768]{1,0:T(8,128)(2,1)S(1)}, bf16[256,768]{1,0:T(8,128)(2,1)S(1)}, u32[]{:S(2)}, u32[]{:S(2)}) collective-permute-start(bf16[256,768]{1,0:T(8,128)(2,1)S(1)} %bitcast_convert_fusion.first_ref), channel_id=1, source_target_pairs={{0,8},{8,0},{16,24},{24,16},{1,9},{9,1},{17,25},{25,17},{2,10},{10... | collective-permute-start | bytes 1179656 | tf_op jit(solution)/shard_map/ppermute | solution.py:1079
  4.0 19.3 %collective-permute-start.4 = (bf16[256,768]{1,0:T(8,128)(2,1)S(1)}, bf16[256,768]{1,0:T(8,128)(2,1)S(1)}, u32[]{:S(2)}, u32[]{:S(2)}) collective-permute-start(bf16[256,768]{1,0:T(8,128)(2,1)S(1)} %bitcast_convert_fusion.first_ref), channel_id=1, source_target_pairs={{0,16},{16,0},{8,24},{24,8},{1,17},{17,1},{9,25},{25,9},{2,18},{18... | collective-permute-start | bytes 1179656 | tf_op jit(solution)/shard_map/ppermute | solution.py:1080
  23.4 61.3 %collective-permute-start.12 = (bf16[1728,768]{1,0:T(8,128)(2,1)}, bf16[1728,768]{1,0:T(8,128)(2,1)}, u32[]{:S(2)}, u32[]{:S(2)}) collective-permute-start(bf16[1728,768]{1,0:T(8,128)(2,1)} %get-tuple-element.191), channel_id=1, source_target_pairs={{0,1},{1,0},{2,3},{3,2},{4,5},{5,4},{6,7},{7,6},{8,9},{9,8},{10,11... | collective-permute-start | bytes 7962632 | tf_op jit(solution)/shard_map/ppermute | solution.py:34
  37.3 14.6 %collective-permute-start.6 = (bf16[512,384]{1,0:T(8,128)(2,1)S(1)}, bf16[512,384]{1,0:T(8,128)(2,1)S(1)}, u32[]{:S(2)}, u32[]{:S(2)}) collective-permute-start(bf16[512,384]{1,0:T(8,128)(2,1)S(1)} %get-tuple-element.188.refs_2_.refs_8_), channel_id=1, source_target_pairs={{0,4},{4,0},{1,5},{5,1},{2,6},{6,2},{3,7},{7,3},{8,12},{12,8},{9,1... | collective-permute-start | bytes 1179656 | tf_op jit(solution)/shard_map/ppermute | solution.py:34
  37.5 20.0 %collective-permute-start.9 = (bf16[512,384]{1,0:T(8,128)(2,1)S(1)}, bf16[512,384]{1,0:T(8,128)(2,1)S(1)}, u32[]{:S(2)}, u32[]{:S(2)}) collective-permute-start(bf16[512,384]{1,0:T(8,128)(2,1)S(1)} %get-tuple-element.189.refs_3_.refs_9_), channel_id=1, source_target_pairs={{0,2},{2,0},{1,3},{3,1},{4,6},{6,4},{5,7},{7,5},{8,10},{10,8},{9,1... | collective-permute-start | bytes 1179656 | tf_op jit(solution)/shard_map/ppermute | solution.py:34
  41.4 16.2 %collective-permute-start.8 = (bf16[512,384]{1,0:T(8,128)(2,1)S(1)}, bf16[512,384]{1,0:T(8,128)(2,1)S(1)}, u32[]{:S(2)}, u32[]{:S(2)}) collective-permute-start(bf16[512,384]{1,0:T(8,128)(2,1)S(1)} %get-tuple-element.188.refs_2_.refs_8_), channel_id=1, source_target_pairs={{0,2},{2,0},{1,3},{3,1},{4,6},{6,4},{5,7},{7,5},{8,10},{10,8},{9,1... | collective-permute-start | bytes 1179656 | tf_op jit(solution)/shard_map/ppermute | solution.py:34
  43.5 14.1 %collective-permute-start.11 = (bf16[512,384]{1,0:T(8,128)(2,1)S(1)}, bf16[512,384]{1,0:T(8,128)(2,1)S(1)}, u32[]{:S(2)}, u32[]{:S(2)}) collective-permute-start(bf16[512,384]{1,0:T(8,128)(2,1)S(1)} %collective-permute-done.7.refs_5_.refs_11_), channel_id=1, source_target_pairs={{0,2},{2,0},{1,3},{3,1},{4,6},{6,4},{5,7},{7,5},{8,10},{10,8},{9,1... | collective-permute-start | bytes 1179656 | tf_op jit(solution)/shard_map/ppermute | solution.py:34
  113.8 13.6 %collective-permute-start.19 = (f32[16,768]{1,0:T(8,128)}, f32[16,768]{1,0:T(8,128)S(1)}, u32[]{:S(2)}, u32[]{:S(2)}) collective-permute-start(f32[16,768]{1,0:T(8,128)} %get-tuple-element.205.own_small_ref), channel_id=1, source_target_pairs={{0,2},{2,0},{1,3},{3,1},{4,6},{6,4},{5,7},{7,5},{8,10},{10,8},{9,1... | collective-permute-start | bytes 147464 | tf_op jit(solution)/shard_map/ppermute | solution.py:34
  113.9 18.0 %collective-permute-start.20 = (bf16[192,256]{1,0:T(8,128)(2,1)}, bf16[192,256]{1,0:T(8,128)(2,1)S(1)}, u32[]{:S(2)}, u32[]{:S(2)}) collective-permute-start(bf16[192,256]{1,0:T(8,128)(2,1)} %get-tuple-element.208), channel_id=1, source_target_pairs={{0,8},{8,0},{16,24},{24,16},{1,9},{9,1},{17,25},{25,17},{2,10},{10... | collective-permute-start | bytes 294920 | tf_op jit(solution)/shard_map/ppermute | solution.py:1069
  115.2 16.8 %collective-permute-start.21 = (bf16[192,256]{1,0:T(8,128)(2,1)}, bf16[192,256]{1,0:T(8,128)(2,1)S(1)}, u32[]{:S(2)}, u32[]{:S(2)}) collective-permute-start(bf16[192,256]{1,0:T(8,128)(2,1)} %get-tuple-element.209), channel_id=1, source_target_pairs={{0,16},{16,0},{8,24},{24,8},{1,17},{17,1},{9,25},{25,9},{2,18},{18... | collective-permute-start | bytes 294920 | tf_op jit(solution)/shard_map/ppermute | solution.py:1069
  115.2 16.7 %collective-permute-start.22 = (bf16[192,256]{1,0:T(8,128)(2,1)}, bf16[192,256]{1,0:T(8,128)(2,1)S(1)}, u32[]{:S(2)}, u32[]{:S(2)}) collective-permute-start(bf16[192,256]{1,0:T(8,128)(2,1)} %get-tuple-element.210), channel_id=1, source_target_pairs={{0,24},{24,0},{8,16},{16,8},{1,25},{25,1},{9,17},{17,9},{2,26},{26... | collective-permute-start | bytes 294920 | tf_op jit(solution)/shard_map/ppermute | solution.py:1069
  132.0 29.3 %collective-permute-start.23 = (bf16[768,768]{1,0:T(8,128)(2,1)}, bf16[768,768]{1,0:T(8,128)(2,1)}, u32[]{:S(2)}, u32[]{:S(2)}) collective-permute-start(bf16[768,768]{1,0:T(8,128)(2,1)} %down_slab.2), channel_id=1, source_target_pairs={{0,1},{1,0},{2,3},{3,2},{4,5},{5,4},{6,7},{7,6},{8,9},{9,8},{10,11... | collective-permute-start | bytes 3538952 | tf_op jit(solution)/shard_map/ppermute | solution.py:34
  132.1 47.8 %collective-permute-start.25 = (bf16[384,2048]{1,0:T(8,128)(2,1)}, bf16[384,2048]{1,0:T(8,128)(2,1)}, u32[]{:S(2)}, u32[]{:S(2)}) collective-permute-start(bf16[384,2048]{1,0:T(8,128)(2,1)} %get-tuple-element.228), channel_id=1, source_target_pairs={{0,4},{4,0},{1,5},{5,1},{2,6},{6,2},{3,7},{7,3},{8,12},{12,8},{9,1... | collective-permute-start | bytes 4718600 | tf_op jit(solution)/shard_map/ppermute | solution.py:34
  133.4 46.4 %collective-permute-start.26 = (bf16[576,768]{1,0:T(8,128)(2,1)}, bf16[576,768]{1,0:T(8,128)(2,1)S(1)}, u32[]{:S(2)}, u32[]{:S(2)}) collective-permute-start(bf16[576,768]{1,0:T(8,128)(2,1)} %get-tuple-element.229), channel_id=1, source_target_pairs={{0,1},{1,0},{2,3},{3,2},{4,5},{5,4},{6,7},{7,6},{8,9},{9,8},{10,11... | collective-permute-start | bytes 2654216 | tf_op jit(solution)/shard_map/ppermute | solution.py:34
  163.9 15.9 %collective-permute-start.24 = (bf16[384,768]{1,0:T(8,128)(2,1)S(1)}, bf16[384,768]{1,0:T(8,128)(2,1)}, u32[]{:S(2)}, u32[]{:S(2)}) collective-permute-start(bf16[384,768]{1,0:T(8,128)(2,1)S(1)} %constant_dynamic-slice_fusion.6), channel_id=1, source_target_pairs={{0,8},{8,0},{16,24},{24,16},{1,9},{9,1},{17,25},{25,17},{2,10},{10... | collective-permute-start | bytes 1769480 | tf_op jit(solution)/shard_map/ppermute | solution.py:1191
  185.2 27.7 %collective-permute-start.30 = (bf16[192,2048]{1,0:T(8,128)(2,1)}, bf16[192,2048]{1,0:T(8,128)(2,1)}, u32[]{:S(2)}, u32[]{:S(2)}) collective-permute-start(bf16[192,2048]{1,0:T(8,128)(2,1)} %dynamic-slice_bitcast_fusion), channel_id=1, source_target_pairs={{0,1},{1,0},{2,3},{3,2},{4,5},{5,4},{6,7},{7,6},{8,9},{9,8},{10,11... | collective-permute-start | bytes 2359304 | tf_op jit(solution)/shard_map/ppermute | solution.py:34
  187.8 25.8 %collective-permute-start.28 = (bf16[1024,384]{1,0:T(8,128)(2,1)}, bf16[1024,384]{1,0:T(8,128)(2,1)}, u32[]{:S(2)}, u32[]{:S(2)}) collective-permute-start(bf16[1024,384]{1,0:T(8,128)(2,1)} %add_convert_fusion.2), channel_id=1, source_target_pairs={{0,4},{4,0},{1,5},{5,1},{2,6},{6,2},{3,7},{7,3},{8,12},{12,8},{9,1... | collective-permute-start | bytes 2359304 | tf_op jit(solution)/shard_map/ppermute | solution.py:34
  190.4 22.5 %collective-permute-start.29 = (bf16[192,768]{1,0:T(8,128)(2,1)}, bf16[192,768]{1,0:T(8,128)(2,1)S(1)}, u32[]{:S(2)}, u32[]{:S(2)}) collective-permute-start(bf16[192,768]{1,0:T(8,128)(2,1)} %constant_dynamic-slice_fusion.5), channel_id=1, source_target_pairs={{0,16},{16,0},{8,24},{24,8},{1,17},{17,1},{9,25},{25,9},{2,18},{18... | collective-permute-start | bytes 884744 | tf_op jit(solution)/shard_map/ppermute | solution.py:1194
  191.8 21.1 %collective-permute-start.32 = (bf16[192,256]{1,0:T(8,128)(2,1)S(1)}, bf16[192,256]{1,0:T(8,128)(2,1)S(1)}, u32[]{:S(2)}, u32[]{:S(2)}) collective-permute-start(bf16[192,256]{1,0:T(8,128)(2,1)S(1)} %copy-done.25), channel_id=1, source_target_pairs={{0,16},{16,0},{8,24},{24,8},{1,17},{17,1},{9,25},{25,9},{2,18},{18... | collective-permute-start | bytes 294920 | tf_op jit(solution)/shard_map/ppermute | solution.py:1069
  199.3 13.6 %collective-permute-start.33 = (bf16[192,256]{1,0:T(8,128)(2,1)S(1)}, bf16[192,256]{1,0:T(8,128)(2,1)S(1)}, u32[]{:S(2)}, u32[]{:S(2)}) collective-permute-start(bf16[192,256]{1,0:T(8,128)(2,1)S(1)} %copy-done.28), channel_id=1, source_target_pairs={{0,24},{24,0},{8,16},{16,8},{1,25},{25,1},{9,17},{17,9},{2,26},{26... | collective-permute-start | bytes 294920 | tf_op jit(solution)/shard_map/ppermute | solution.py:1069
  224.3 18.8 %collective-permute-start.36 = (bf16[96,2048]{1,0:T(8,128)(2,1)}, bf16[96,2048]{1,0:T(8,128)(2,1)}, u32[]{:S(2)}, u32[]{:S(2)}) collective-permute-start(bf16[96,2048]{1,0:T(8,128)(2,1)} %constant_dynamic-slice_fusion.4), channel_id=1, source_target_pairs={{0,8},{8,0},{16,24},{24,16},{1,9},{9,1},{17,25},{25,17},{2,10},{10... | collective-permute-start | bytes 1179656 | tf_op jit(solution)/shard_map/ppermute | solution.py:1191
  226.7 24.6 %collective-permute-start.38 = (bf16[384,256]{1,0:T(8,128)(2,1)}, bf16[384,256]{1,0:T(8,128)(2,1)S(1)}, u32[]{:S(2)}, u32[]{:S(2)}) collective-permute-start(bf16[384,256]{1,0:T(8,128)(2,1)} %copy-done.22), channel_id=1, source_target_pairs={{0,8},{8,0},{16,24},{24,16},{1,9},{9,1},{17,25},{25,17},{2,10},{10... | collective-permute-start | bytes 589832 | tf_op jit(solution)/shard_map/ppermute | solution.py:1069
  226.7 25.5 %collective-permute-start.39 = (bf16[384,256]{1,0:T(8,128)(2,1)}, bf16[384,256]{1,0:T(8,128)(2,1)S(1)}, u32[]{:S(2)}, u32[]{:S(2)}) collective-permute-start(bf16[384,256]{1,0:T(8,128)(2,1)} %copy-done.20), channel_id=1, source_target_pairs={{0,16},{16,0},{8,24},{24,8},{1,17},{17,1},{9,25},{25,9},{2,18},{18... | collective-permute-start | bytes 589832 | tf_op jit(solution)/shard_map/ppermute | solution.py:1069
  228.9 23.8 %collective-permute-start.40 = (bf16[384,256]{1,0:T(8,128)(2,1)}, bf16[384,256]{1,0:T(8,128)(2,1)S(1)}, u32[]{:S(2)}, u32[]{:S(2)}) collective-permute-start(bf16[384,256]{1,0:T(8,128)(2,1)} %copy-done.18), channel_id=1, source_target_pairs={{0,24},{24,0},{8,16},{16,8},{1,25},{25,1},{9,17},{17,9},{2,26},{26... | collective-permute-start | bytes 589832 | tf_op jit(solution)/shard_map/ppermute | solution.py:1069
  231.3 30.6 %collective-permute-start.42 = (bf16[96,768]{1,0:T(8,128)(2,1)S(1)}, bf16[96,768]{1,0:T(8,128)(2,1)S(1)}, u32[]{:S(2)}, u32[]{:S(2)}) collective-permute-start(bf16[96,768]{1,0:T(8,128)(2,1)S(1)} %add_convert_fusion.9), channel_id=1, source_target_pairs={{0,16},{16,0},{8,24},{24,8},{1,17},{17,1},{9,25},{25,9},{2,18},{18... | collective-permute-start | bytes 442376 | tf_op jit(solution)/shard_map/ppermute | solution.py:1194
  251.3 36.9 %collective-permute-start.49 = (bf16[576,768]{1,0:T(8,128)(2,1)S(1)}, bf16[576,768]{1,0:T(8,128)(2,1)S(1)}, u32[]{:S(2)}, u32[]{:S(2)}) collective-permute-start(bf16[576,768]{1,0:T(8,128)(2,1)S(1)} %copy-done.35), channel_id=1, source_target_pairs={{0,2},{2,0},{1,3},{3,1},{4,6},{6,4},{5,7},{7,5},{8,10},{10,8},{9,1... | collective-permute-start | bytes 2654216 | tf_op jit(solution)/shard_map/ppermute | solution.py:34
  261.9 13.8 %collective-permute-start.45 = (bf16[2,96,768]{2,1,0:T(8,128)(2,1)S(1)}, bf16[2,96,768]{2,1,0:T(8,128)(2,1)S(1)}, u32[]{:S(2)}, u32[]{:S(2)}) collective-permute-start(bf16[2,96,768]{2,1,0:T(8,128)(2,1)S(1)} %maximum_select_fusion.5), channel_id=1, source_target_pairs={{0,8},{8,0},{16,24},{24,16},{1,9},{9,1},{17,25},{25,17},{2,10},{10... | collective-permute-start | bytes 884744 | tf_op jit(solution)/shard_map/ppermute | solution.py:1191
  264.5 19.9 %collective-permute-start.46 = (bf16[208,640]{1,0:T(8,128)(2,1)S(1)}, bf16[208,640]{1,0:T(8,128)(2,1)S(1)}, u32[]{:S(2)}, u32[]{:S(2)}) collective-permute-start(bf16[208,640]{1,0:T(8,128)(2,1)S(1)} %add_convert_fusion.6), channel_id=1, source_target_pairs={{0,16},{16,0},{8,24},{24,8},{1,17},{17,1},{9,25},{25,9},{2,18},{18... | collective-permute-start | bytes 798728 | tf_op jit(solution)/shard_map/ppermute | solution.py:1194
  272.2 15.3 %collective-permute-start.47 = (bf16[96,2048]{1,0:T(8,128)(2,1)S(1)}, bf16[96,2048]{1,0:T(8,128)(2,1)S(1)}, u32[]{:S(2)}, u32[]{:S(2)}) collective-permute-start(bf16[96,2048]{1,0:T(8,128)(2,1)S(1)} %maximum_select_fusion.4), channel_id=1, source_target_pairs={{0,8},{8,0},{16,24},{24,16},{1,9},{9,1},{17,25},{25,17},{2,10},{10... | collective-permute-start | bytes 1179656 | tf_op jit(solution)/shard_map/ppermute | solution.py:1191
  275.9 20.9 %collective-permute-start.48 = (bf16[384,768]{1,0:T(8,128)(2,1)S(1)}, bf16[384,768]{1,0:T(8,128)(2,1)S(1)}, u32[]{:S(2)}, u32[]{:S(2)}) collective-permute-start(bf16[384,768]{1,0:T(8,128)(2,1)S(1)} %bitcast.47), channel_id=1, source_target_pairs={{0,4},{4,0},{1,5},{5,1},{2,6},{6,2},{3,7},{7,3},{8,12},{12,8},{9,1... | collective-permute-start | bytes 1769480 | tf_op jit(solution)/shard_map/ppermute | solution.py:34
  284.6 14.4 %collective-permute-start.50 = (bf16[416,640]{1,0:T(8,128)(2,1)S(1)}, bf16[416,640]{1,0:T(8,128)(2,1)S(1)}, u32[]{:S(2)}, u32[]{:S(2)}) collective-permute-start(bf16[416,640]{1,0:T(8,128)(2,1)S(1)} %maximum_select_fusion.3), channel_id=1, source_target_pairs={{0,8},{8,0},{16,24},{24,16},{1,9},{9,1},{17,25},{25,17},{2,10},{10... | collective-permute-start | bytes 1597448 | tf_op jit(solution)/shard_map/ppermute | solution.py:1191
  287.6 17.2 %collective-permute-start.51 = (bf16[192,2048]{1,0:T(8,128)(2,1)S(1)}, bf16[192,2048]{1,0:T(8,128)(2,1)}, u32[]{:S(2)}, u32[]{:S(2)}) collective-permute-start(bf16[192,2048]{1,0:T(8,128)(2,1)S(1)} %maximum_select_fusion.1.refs_0_), channel_id=1, source_target_pairs={{0,4},{4,0},{1,5},{5,1},{2,6},{6,2},{3,7},{7,3},{8,12},{12,8},{9,1... | collective-permute-start | bytes 2359304 | tf_op jit(solution)/shard_map/ppermute | solution.py:34
  (104 other events, 869.5 us)
where the time goes:
time: 325 us; the launch traced here: 319 us
  Pallas kernels  128 us (39%)
  starting transfers between devices  77.4 us (24%)
  waiting for transfers between devices  73.7 us (23%)
  local copies, waits for them, and re-layouts  23.6 us (7%)
  other arithmetic  14 us (4%)
    ppermute x32, starting transfers between devices, swap(): return lax.ppermute(value, axis, SWAP)  46.3 us
    pallas_call x2, Pallas kernels, attend_backward(): pl.pallas_call(partial(backward_kernel, blocks=blocks, rows=2 * half_rows...  41 us
    pallas_call x1, Pallas kernels, attend_forward(): pl.pallas_call(partial(forward_kernel, blocks=blocks, rows=2 * half_rows...  25.9 us
    ppermute x5, waiting for transfers between devices, to_far(): return lax.ppermute(value, 'z', far)  24.4 us
    ppermute x12, waiting for transfers between devices, exchange(): lax.ppermute(item, 'z', perm)  19.4 us
    unnamed x158, local copies, waits for them, and re-layouts  16.6 us
    pallas_call x1, Pallas kernels, middle(): pl.pallas_call(partial(middle_kernel, groups=groups, shared=len(weights)...  15.9 us
    ppermute x12, starting transfers between devices, exchange(): lax.ppermute(item, 'z', perm)  14.4 us
  transfers between devices with their start and end apart: 57, of which 20 were waited for; matrix products, arithmetic and copies ran while one was open for 5% of the time, Pallas kernels for 32%

commit v1 on v0

--- a/solution.py
+++ b/solution.py
@@ -1245,8 +1245,10 @@
         down_sum = add_pair(part_of(down_sum, x_at, 2, 0), down_got)
         down_got = to_far(down_sum)
         head_core = arrive(head_core)
-        head_sent = swap(head_part((1 - w_at,), c_at, head_core), "w")
-        head_sum = head_part((1 * w_at,), c_at, head_core, 1)
+        head_both = head_part((1 - w_at, 1 * w_at), c_at, head_core)
+        head_rows = head_both.shape[0] // 2
+        head_sent = swap(head_both[:head_rows], "w")
+        head_sum = head_both[head_rows:]
         up_got = arrive(up_got)
         up_sum = add_pair(part_of(up_sum, near_bit, 2, 0), up_got)
         up_got = to_far(part_of(up_sum, 1 - far_bit, 2, 0))

time: 325 us -> 320 us (0.985); the launches traced: 319 us -> 319 us
  Pallas kernels: 128 us -> 99.4 us
  starting transfers between devices: 77.4 us -> 91.3 us
  waiting for transfers between devices: 73.7 us -> 84.4 us
  local copies, waits for them, and re-layouts: 23.6 us -> 27 us
    ppermute x32, waiting for transfers between devices: 12.5 us -> 33.6 us  [swap(): return lax.ppermute(value, axis, SWAP)]
    pallas_call x2, Pallas kernels: 41 us -> 24.9 us  [attend_backward(): pl.pallas_call(partial(backward_kernel, blocks=blocks, rows=2 * half_rows...]
    ppermute x32, starting transfers between devices: 46.3 us -> 61.9 us  [swap(): return lax.ppermute(value, axis, SWAP)]
    ppermute x5, waiting for transfers between devices: 12.5 us -> 1.34 us  [to_near(): return lax.ppermute(value, 'z', near)]
    pallas_call x1, Pallas kernels: 25.9 us -> 15 us  [attend_forward(): pl.pallas_call(partial(forward_kernel, blocks=blocks, rows=2 * half_rows...]
    unnamed x158 -> x156, local copies, waits for them, and re-layouts: 16.6 us -> 19.3 us
  transfers between devices with their start and end apart: 57 -> 57, of which waited for: 20 -> 18; matrix products, arithmetic and copies ran while one was open for 5% -> 5% of each run, Pallas kernels for 32% -> 23%
where the time goes in v1:
time: 320 us; the launch traced here: 319 us
  Pallas kernels  99.4 us (31%)
  starting transfers between devices  91.3 us (29%)
  waiting for transfers between devices  84.4 us (26%)
  local copies, waits for them, and re-layouts  27 us (8%)
  other arithmetic  14.5 us (5%)
    ppermute x32, starting transfers between devices, swap(): return lax.ppermute(value, axis, SWAP)  61.9 us
    ppermute x32, waiting for transfers between devices, swap(): return lax.ppermute(value, axis, SWAP)  33.6 us
    pallas_call x2, Pallas kernels, attend_backward(): pl.pallas_call(partial(backward_kernel, blocks=blocks, rows=2 * half_rows...  24.9 us
    ppermute x5, waiting for transfers between devices, to_far(): return lax.ppermute(value, 'z', far)  24.8 us
    ppermute x12, waiting for transfers between devices, exchange(): lax.ppermute(item, 'z', perm)  19.7 us
    unnamed x156, local copies, waits for them, and re-layouts  19.3 us
    pallas_call x1, Pallas kernels, middle(): pl.pallas_call(partial(middle_kernel, groups=groups, shared=len(weights)...  15.9 us
    pallas_call x1, Pallas kernels, attend_forward(): pl.pallas_call(partial(forward_kernel, blocks=blocks, rows=2 * half_rows...  15 us
  transfers between devices with their start and end apart: 57, of which 18 were waited for; matrix products, arithmetic and copies ran while one was open for 5% of the time, Pallas kernels for 23%

profile of v1, /device:TPU:1, one launch (start us, length us, event | category | flops | bytes accessed | tf_op | source)
XLA Modules:
  0.0 318.9 jit_solution(5842909933939394671)
XLA Ops:
  6.9 4.6 %prepare.1 = (bf16[384,384]{1,0:T(8,128)(2,1)}, bf16[384,192]{1,0:T(8,128)(2,1)}, bf16[384,768]{1,0:T(8,128)(2,1)}, bf16[384,768]{1,0:T(8,128)(2,1)}, bf16[384,7...) custom-call(s32[2]{0:T(128)} %get-tuple-element.342.meta_ref, f32[384,768]{1,0:T(8,128)} %refs_0_.1, f32[384,768]{1,0:T(8,128)} %refs_1_.1, ...), custom_call_target="tpu_custom_call" | custom-call | flops 1000 | bytes 1 | tf_op jit(solution)/shard_map/prepare/pallas_call | solution.py:366
  14.5 8.3 %round_weights.1 = (bf16[384,768]{1,0:T(8,128)(2,1)}, bf16[384,3072]{1,0:T(8,128)(2,1)}, bf16[1536,768]{1,0:T(8,128)(2,1)}, bf16[1728,768]{1,0:T(8,128)(2,1)}) custom-call(s32[2]{0:T(128)} %get-tuple-element.342.meta_ref, f32[384,768]{1,0:T(8,128)} %out_w.1, f32[384,3072]{1,0:T(8,128)} %up_w.1, f32[1536,768]{1,0:T(8,128)} %down_w.1), custom_call_target="tpu_custom_call" | custom-call | flops 1000 | bytes 1 | tf_op jit(solution)/shard_map/round_weights/pallas_call | solution.py:264
  28.0 4.9 %collective-permute-done.5.second_ref = bf16[256,768]{1,0:T(8,128)(2,1)S(1)} collective-permute-done((bf16[256,768]{1,0:T(8,128)(2,1)S(1)}, bf16[256,768]{1,0:T(8,128)(2,1)S(1)}, u32[]{:S(2)}, u32[]{:S(2)}) %collective-permute-start.5) | collective-permute-done | bytes 393248 | tf_op jit(solution)/shard_map/ppermute | solution.py:1122
  37.5 3.8 %collective-permute-start.9 = (bf16[512,384]{1,0:T(8,128)(2,1)S(1)}, bf16[512,384]{1,0:T(8,128)(2,1)S(1)}, u32[]{:S(2)}, u32[]{:S(2)}) collective-permute-start(bf16[512,384]{1,0:T(8,128)(2,1)S(1)} %get-tuple-element.189.refs_3_.refs_9_), channel_id=1, source_target_pairs={{0,2},{2,0},{1,3},{3,1},{4,6},{6,4},{5,7},{7,5},{8,10},{10,8},{9,1... | collective-permute-start | bytes 1179656 | tf_op jit(solution)/shard_map/ppermute | solution.py:34
  43.5 7.9 %collective-permute-start.11 = (bf16[512,384]{1,0:T(8,128)(2,1)S(1)}, bf16[512,384]{1,0:T(8,128)(2,1)S(1)}, u32[]{:S(2)}, u32[]{:S(2)}) collective-permute-start(bf16[512,384]{1,0:T(8,128)(2,1)S(1)} %collective-permute-done.7.refs_5_.refs_11_), channel_id=1, source_target_pairs={{0,2},{2,0},{1,3},{3,1},{4,6},{6,4},{5,7},{7,5},{8,10},{10,8},{9,1... | collective-permute-start | bytes 1179656 | tf_op jit(solution)/shard_map/ppermute | solution.py:34
  51.9 4.1 %collective-permute-start.10 = (bf16[512,384]{1,0:T(8,128)(2,1)S(1)}, bf16[512,384]{1,0:T(8,128)(2,1)S(1)}, u32[]{:S(2)}, u32[]{:S(2)}) collective-permute-start(bf16[512,384]{1,0:T(8,128)(2,1)S(1)} %collective-permute-done.6.refs_4_.refs_10_), channel_id=1, source_target_pairs={{0,2},{2,0},{1,3},{3,1},{4,6},{6,4},{5,7},{7,5},{8,10},{10,8},{9,1... | collective-permute-start | bytes 1179656 | tf_op jit(solution)/shard_map/ppermute | solution.py:34
  58.7 15.0 %attend_forward.1 = (f32[192,1024]{1,0:T(8,128)}, bf16[192,256]{1,0:T(8,128)(2,1)}, bf16[192,256]{1,0:T(8,128)(2,1)}, bf16[192,256]{1,0:T(8,128)(2,1)}, bf16[192,256]{1,0:T(8,128)(2,1)}, /*index=5*/f32[3,1,1024]{2,1,0:T(1,128)}) custom-call(s32[6]{0:T(128)} %stack.99.meta_ref, bf16[192,512]{1,0:T(8,128)(2,1)} %copy-done.15, bf16[192,512]{1,0:T(8,128)(2,1)} %copy-done.16, ...), custom_call_target="tpu_custom_call" | custom-call | flops 24000 | bytes 1 | tf_op jit(solution)/shard_map/attend_forward/pallas_call | solution.py:125
  73.7 6.9 %collective-permute-done.12.refs_7_ = bf16[1728,768]{1,0:T(8,128)(2,1)} collective-permute-done((bf16[1728,768]{1,0:T(8,128)(2,1)}, bf16[1728,768]{1,0:T(8,128)(2,1)}, u32[]{:S(2)}, u32[]{:S(2)}) %collective-permute-start.12) | collective-permute-done | bytes 2654240 | tf_op jit(solution)/shard_map/ppermute | solution.py:34
  80.6 3.1 collective-permute-start.17
  84.8 3.1 collective-permute-start.16
  94.7 15.9 %middle.1 = (f32[256,768]{1,0:T(8,128)}, f32[256,768]{1,0:T(8,128)}, bf16[192,256]{1,0:T(8,128)(2,1)}, bf16[192,256]{1,0:T(8,128)(2,1)}, bf16[192,256]{1,0:T(8,1...) custom-call(s32[4]{0:T(128)} %pad_add_fusion.2.meta_ref, ...), custom_call_target="tpu_custom_call" | custom-call | flops 15000 | bytes 1 | tf_op jit(solution)/shard_map/middle/pallas_call | solution.py:641
  126.5 2.9 up_slabs.1
  133.6 15.7 %attend_backward.2 = (bf16[192,256]{1,0:T(8,128)(2,1)}, bf16[192,256]{1,0:T(8,128)(2,1)}, bf16[192,256]{1,0:T(8,128)(2,1)}, bf16[192,256]{1,0:T(8,128)(2,1)}, bf...) custom-call(s32[6]{0:T(128)} %stack.99.meta_ref, bf16[192,512]{1,0:T(8,128)(2,1)} %copy-done.15, ...), custom_call_target="tpu_custom_call" | custom-call | flops 24000 | bytes 1 | tf_op jit(solution)/shard_map/attend_backward/pallas_call | solution.py:226
  149.3 9.1 %collective-permute-done.23 = bf16[768,768]{1,0:T(8,128)(2,1)S(1)} collective-permute-done((bf16[768,768]{1,0:T(8,128)(2,1)}, bf16[768,768]{1,0:T(8,128)(2,1)S(1)}, u32[]{:S(2)}, u32[]{:S(2)}) %collective-permute-start.23) | collective-permute-done | bytes 1179680 | tf_op jit(solution)/shard_map/ppermute | solution.py:34
  163.5 9.2 %attend_backward.3 = (bf16[192,256]{1,0:T(8,128)(2,1)}, bf16[192,256]{1,0:T(8,128)(2,1)}, bf16[192,256]{1,0:T(8,128)(2,1)}, bf16[192,256]{1,0:T(8,128)(2,1)}, bf...) custom-call(s32[6]{0:T(128)} %stack.99.meta_ref, ...), custom_call_target="tpu_custom_call", output_to_operand_aliasing={{0}: (17, {}), {1}: (18, {}), {2}: (19, {}), {3}: (20, {}),... | custom-call | flops 12000 | bytes 1 | tf_op jit(solution)/shard_map/attend_backward/pallas_call | solution.py:226
  172.7 4.6 %collective-permute-done.26.refs_11_ = bf16[576,768]{1,0:T(8,128)(2,1)S(1)} collective-permute-done((bf16[576,768]{1,0:T(8,128)(2,1)}, bf16[576,768]{1,0:T(8,128)(2,1)S(1)}, u32[]{:S(2)}, u32[]{:S(2)}) %collective-permute-start.26) | collective-permute-done | bytes 884768 | tf_op jit(solution)/shard_map/ppermute | solution.py:34
  182.4 4.2 %collective-permute-start.30 = (bf16[192,2048]{1,0:T(8,128)(2,1)}, bf16[192,2048]{1,0:T(8,128)(2,1)}, u32[]{:S(2)}, u32[]{:S(2)}) collective-permute-start(bf16[192,2048]{1,0:T(8,128)(2,1)} %dynamic-slice_bitcast_fusion), channel_id=1, source_target_pairs={{0,1},{1,0},{2,3},{3,2},{4,5},{5,4},{6,7},{7,6},{8,9},{9,8},{10,11... | collective-permute-start | bytes 2359304 | tf_op jit(solution)/shard_map/ppermute | solution.py:34
  192.9 5.7 %collective-permute-done.31.refs_1_ = bf16[192,256]{1,0:T(8,128)(2,1)S(1)} collective-permute-done((bf16[192,256]{1,0:T(8,128)(2,1)S(1)}, bf16[192,256]{1,0:T(8,128)(2,1)S(1)}, u32[]{:S(2)}, u32[]{:S(2)}) %collective-permute-start.31) | collective-permute-done | bytes 98336 | tf_op jit(solution)/shard_map/ppermute | solution.py:1069
  200.9 12.1 %collective-permute-done.32.refs_2_ = bf16[192,256]{1,0:T(8,128)(2,1)S(1)} collective-permute-done((bf16[192,256]{1,0:T(8,128)(2,1)S(1)}, bf16[192,256]{1,0:T(8,128)(2,1)S(1)}, u32[]{:S(2)}, u32[]{:S(2)}) %collective-permute-start.32) | collective-permute-done | bytes 98336 | tf_op jit(solution)/shard_map/ppermute | solution.py:1069
  228.5 2.8 collective-permute-done.34
  241.3 3.7 %collective-permute-done.37 = bf16[208,640]{1,0:T(8,128)(2,1)S(1)} collective-permute-done((bf16[208,640]{1,0:T(8,128)(2,1)S(1)}, bf16[208,640]{1,0:T(8,128)(2,1)S(1)}, u32[]{:S(2)}, u32[]{:S(2)}) %collective-permute-start.37) | collective-permute-done | bytes 266272 | tf_op jit(solution)/shard_map/ppermute | solution.py:34
  247.2 3.0 collective-permute-start.49
  251.5 10.0 %collective-permute-done.41 = bf16[48,2048]{1,0:T(8,128)(2,1)S(1)} collective-permute-done((bf16[48,2048]{1,0:T(8,128)(2,1)S(1)}, bf16[48,2048]{1,0:T(8,128)(2,1)S(1)}, u32[]{:S(2)}, u32[]{:S(2)}) %collective-permute-start.41) | collective-permute-done | bytes 196640 | tf_op jit(solution)/shard_map/ppermute | solution.py:1194
  264.3 6.6 %collective-permute-done.44 = bf16[48,2048]{1,0:T(8,128)(2,1)S(1)} collective-permute-done((bf16[48,2048]{1,0:T(8,128)(2,1)S(1)}, bf16[48,2048]{1,0:T(8,128)(2,1)S(1)}, u32[]{:S(2)}, u32[]{:S(2)}) %collective-permute-start.44) | collective-permute-done | bytes 196640 | tf_op jit(solution)/shard_map/ppermute | solution.py:1194
  275.0 8.2 %collective-permute-done.46 = bf16[208,640]{1,0:T(8,128)(2,1)S(1)} collective-permute-done((bf16[208,640]{1,0:T(8,128)(2,1)S(1)}, bf16[208,640]{1,0:T(8,128)(2,1)S(1)}, u32[]{:S(2)}, u32[]{:S(2)}) %collective-permute-start.46) | collective-permute-done | bytes 266272 | tf_op jit(solution)/shard_map/ppermute | solution.py:1194
  283.8 3.8 %token_gradient.1 = f32[256,768]{1,0:T(8,128)} custom-call(s32[4]{0:T(128)S(1)} %copy-done.48, f32[256,768]{1,0:T(8,128)S(1)} %copy-done.30, bf16[192,256]{1,0:T(8,128)(2,1)S(1)} %copy-done.17, bf16[192,256]{1,0:T(8,128)(2,1)S(1)} %copy-done.42, bf16[192,256]{1,0:T(8,128)(2,1)S(1)} %copy-done.44, bf16[192,256]{1,0:T(8,128)(2,1)S(1)} %copy-done.46, ...), custom_call_target="tpu_custom_call" | custom-call | flops 4000 | bytes 1 | tf_op jit(solution)/shard_map/token_gradient/pallas_call | solution.py:889
  287.6 10.2 %collective-permute-start.52 = (bf16[384,768]{1,0:T(8,128)(2,1)S(1)}, bf16[384,768]{1,0:T(8,128)(2,1)S(1)}, u32[]{:S(2)}, u32[]{:S(2)}) collective-permute-start(bf16[384,768]{1,0:T(8,128)(2,1)S(1)} %bitcast.48), channel_id=1, source_target_pairs={{0,2},{2,0},{1,3},{3,1},{4,6},{6,4},{5,7},{7,5},{8,10},{10,8},{9,1... | collective-permute-start | bytes 1769480 | tf_op jit(solution)/shard_map/ppermute | solution.py:34
  298.3 3.4 %collective-permute-start.54 = (bf16[832,640]{1,0:T(8,128)(2,1)S(1)}, bf16[832,640]{1,0:T(8,128)(2,1)S(1)}, u32[]{:S(2)}, u32[]{:S(2)}) collective-permute-start(bf16[832,640]{1,0:T(8,128)(2,1)S(1)} %maximum_select_fusion.own_ref), channel_id=1, source_target_pairs={{0,2},{2,0},{1,3},{3,1},{4,6},{6,4},{5,7},{7,5},{8,10},{10,8},{9,1... | collective-permute-start | bytes 3194888 | tf_op jit(solution)/shard_map/ppermute | solution.py:34
  301.8 3.0 down_finish.1
  304.8 3.8 %collective-permute-start.56 = (bf16[192,2048]{1,0:T(8,128)(2,1)}, bf16[192,2048]{1,0:T(8,128)(2,1)}, u32[]{:S(2)}, u32[]{:S(2)}) collective-permute-start(bf16[192,2048]{1,0:T(8,128)(2,1)} %collective-permute-done.51.refs_1_), channel_id=1, source_target_pairs={{0,2},{2,0},{1,3},{3,1},{4,6},{6,4},{5,7},{7,5},{8,10},{10,8},{9,1... | collective-permute-start | bytes 2359304 | tf_op jit(solution)/shard_map/ppermute | solution.py:34
  308.6 2.7 head_finish.1
  312.6 5.1 %up_finish.1 = (f32[384,3072]{1,0:T(8,128)}, f32[384,768]{1,0:T(8,128)}, f32[384,128]{1,0:T(8,128)S(1)}) custom-call(s32[2]{0:T(128)S(1)} %pad_add_fusion.5.meta_ref, bf16[192,2048]{1,0:T(8,128)(2,1)S(1)} %maximum_select_fusion.1.refs_0_, bf16[192,2048]{1,0:T(8,128)(2,1)} %collective-permute-done.51.refs_1_, ...), custom_call_target="tpu_custom_call" | custom-call | flops 5000 | bytes 1 | tf_op jit(solution)/shard_map/up_finish/pallas_call | solution.py:959
  (317 shorter events, 109.1 us)
Async XLA Ops:
  1.8 21.5 %collective-permute-start.3 = (bf16[256,768]{1,0:T(8,128)(2,1)S(1)}, bf16[256,768]{1,0:T(8,128)(2,1)S(1)}, u32[]{:S(2)}, u32[]{:S(2)}) collective-permute-start(bf16[256,768]{1,0:T(8,128)(2,1)S(1)} %bitcast_convert_fusion.first_ref), channel_id=1, source_target_pairs={{0,8},{8,0},{16,24},{24,16},{1,9},{9,1},{17,25},{25,17},{2,10},{10... | collective-permute-start | bytes 1179656 | tf_op jit(solution)/shard_map/ppermute | solution.py:1079
  4.0 19.3 %collective-permute-start.4 = (bf16[256,768]{1,0:T(8,128)(2,1)S(1)}, bf16[256,768]{1,0:T(8,128)(2,1)S(1)}, u32[]{:S(2)}, u32[]{:S(2)}) collective-permute-start(bf16[256,768]{1,0:T(8,128)(2,1)S(1)} %bitcast_convert_fusion.first_ref), channel_id=1, source_target_pairs={{0,16},{16,0},{8,24},{24,8},{1,17},{17,1},{9,25},{25,9},{2,18},{18... | collective-permute-start | bytes 1179656 | tf_op jit(solution)/shard_map/ppermute | solution.py:1080
  23.4 57.3 %collective-permute-start.12 = (bf16[1728,768]{1,0:T(8,128)(2,1)}, bf16[1728,768]{1,0:T(8,128)(2,1)}, u32[]{:S(2)}, u32[]{:S(2)}) collective-permute-start(bf16[1728,768]{1,0:T(8,128)(2,1)} %get-tuple-element.191), channel_id=1, source_target_pairs={{0,1},{1,0},{2,3},{3,2},{4,5},{5,4},{6,7},{7,6},{8,9},{9,8},{10,11... | collective-permute-start | bytes 7962632 | tf_op jit(solution)/shard_map/ppermute | solution.py:34
  37.3 14.6 %collective-permute-start.6 = (bf16[512,384]{1,0:T(8,128)(2,1)S(1)}, bf16[512,384]{1,0:T(8,128)(2,1)S(1)}, u32[]{:S(2)}, u32[]{:S(2)}) collective-permute-start(bf16[512,384]{1,0:T(8,128)(2,1)S(1)} %get-tuple-element.188.refs_2_.refs_8_), channel_id=1, source_target_pairs={{0,4},{4,0},{1,5},{5,1},{2,6},{6,2},{3,7},{7,3},{8,12},{12,8},{9,1... | collective-permute-start | bytes 1179656 | tf_op jit(solution)/shard_map/ppermute | solution.py:34
  37.5 20.0 %collective-permute-start.9 = (bf16[512,384]{1,0:T(8,128)(2,1)S(1)}, bf16[512,384]{1,0:T(8,128)(2,1)S(1)}, u32[]{:S(2)}, u32[]{:S(2)}) collective-permute-start(bf16[512,384]{1,0:T(8,128)(2,1)S(1)} %get-tuple-element.189.refs_3_.refs_9_), channel_id=1, source_target_pairs={{0,2},{2,0},{1,3},{3,1},{4,6},{6,4},{5,7},{7,5},{8,10},{10,8},{9,1... | collective-permute-start | bytes 1179656 | tf_op jit(solution)/shard_map/ppermute | solution.py:34
  41.4 16.2 %collective-permute-start.8 = (bf16[512,384]{1,0:T(8,128)(2,1)S(1)}, bf16[512,384]{1,0:T(8,128)(2,1)S(1)}, u32[]{:S(2)}, u32[]{:S(2)}) collective-permute-start(bf16[512,384]{1,0:T(8,128)(2,1)S(1)} %get-tuple-element.188.refs_2_.refs_8_), channel_id=1, source_target_pairs={{0,2},{2,0},{1,3},{3,1},{4,6},{6,4},{5,7},{7,5},{8,10},{10,8},{9,1... | collective-permute-start | bytes 1179656 | tf_op jit(solution)/shard_map/ppermute | solution.py:34
  43.5 14.1 %collective-permute-start.11 = (bf16[512,384]{1,0:T(8,128)(2,1)S(1)}, bf16[512,384]{1,0:T(8,128)(2,1)S(1)}, u32[]{:S(2)}, u32[]{:S(2)}) collective-permute-start(bf16[512,384]{1,0:T(8,128)(2,1)S(1)} %collective-permute-done.7.refs_5_.refs_11_), channel_id=1, source_target_pairs={{0,2},{2,0},{1,3},{3,1},{4,6},{6,4},{5,7},{7,5},{8,10},{10,8},{9,1... | collective-permute-start | bytes 1179656 | tf_op jit(solution)/shard_map/ppermute | solution.py:34
  112.4 13.6 %collective-permute-start.19 = (f32[16,768]{1,0:T(8,128)}, f32[16,768]{1,0:T(8,128)S(1)}, u32[]{:S(2)}, u32[]{:S(2)}) collective-permute-start(f32[16,768]{1,0:T(8,128)} %get-tuple-element.205.own_small_ref), channel_id=1, source_target_pairs={{0,2},{2,0},{1,3},{3,1},{4,6},{6,4},{5,7},{7,5},{8,10},{10,8},{9,1... | collective-permute-start | bytes 147464 | tf_op jit(solution)/shard_map/ppermute | solution.py:34
  112.5 18.0 %collective-permute-start.20 = (bf16[192,256]{1,0:T(8,128)(2,1)}, bf16[192,256]{1,0:T(8,128)(2,1)S(1)}, u32[]{:S(2)}, u32[]{:S(2)}) collective-permute-start(bf16[192,256]{1,0:T(8,128)(2,1)} %get-tuple-element.208), channel_id=1, source_target_pairs={{0,8},{8,0},{16,24},{24,16},{1,9},{9,1},{17,25},{25,17},{2,10},{10... | collective-permute-start | bytes 294920 | tf_op jit(solution)/shard_map/ppermute | solution.py:1069
  114.1 16.4 %collective-permute-start.21 = (bf16[192,256]{1,0:T(8,128)(2,1)}, bf16[192,256]{1,0:T(8,128)(2,1)S(1)}, u32[]{:S(2)}, u32[]{:S(2)}) collective-permute-start(bf16[192,256]{1,0:T(8,128)(2,1)} %get-tuple-element.209), channel_id=1, source_target_pairs={{0,16},{16,0},{8,24},{24,8},{1,17},{17,1},{9,25},{25,9},{2,18},{18... | collective-permute-start | bytes 294920 | tf_op jit(solution)/shard_map/ppermute | solution.py:1069
  114.1 16.4 %collective-permute-start.22 = (bf16[192,256]{1,0:T(8,128)(2,1)}, bf16[192,256]{1,0:T(8,128)(2,1)S(1)}, u32[]{:S(2)}, u32[]{:S(2)}) collective-permute-start(bf16[192,256]{1,0:T(8,128)(2,1)} %get-tuple-element.210), channel_id=1, source_target_pairs={{0,24},{24,0},{8,16},{16,8},{1,25},{25,1},{9,17},{17,9},{2,26},{26... | collective-permute-start | bytes 294920 | tf_op jit(solution)/shard_map/ppermute | solution.py:1069
  130.6 27.8 %collective-permute-start.23 = (bf16[768,768]{1,0:T(8,128)(2,1)}, bf16[768,768]{1,0:T(8,128)(2,1)S(1)}, u32[]{:S(2)}, u32[]{:S(2)}) collective-permute-start(bf16[768,768]{1,0:T(8,128)(2,1)} %down_slab.2), channel_id=1, source_target_pairs={{0,1},{1,0},{2,3},{3,2},{4,5},{5,4},{6,7},{7,6},{8,9},{9,8},{10,11... | collective-permute-start | bytes 3538952 | tf_op jit(solution)/shard_map/ppermute | solution.py:34
  132.2 45.0 %collective-permute-start.25 = (bf16[384,2048]{1,0:T(8,128)(2,1)}, bf16[384,2048]{1,0:T(8,128)(2,1)}, u32[]{:S(2)}, u32[]{:S(2)}) collective-permute-start(bf16[384,2048]{1,0:T(8,128)(2,1)} %get-tuple-element.228), channel_id=1, source_target_pairs={{0,4},{4,0},{1,5},{5,1},{2,6},{6,2},{3,7},{7,3},{8,12},{12,8},{9,1... | collective-permute-start | bytes 4718600 | tf_op jit(solution)/shard_map/ppermute | solution.py:34
  133.5 43.8 %collective-permute-start.26 = (bf16[576,768]{1,0:T(8,128)(2,1)}, bf16[576,768]{1,0:T(8,128)(2,1)S(1)}, u32[]{:S(2)}, u32[]{:S(2)}) collective-permute-start(bf16[576,768]{1,0:T(8,128)(2,1)} %get-tuple-element.229), channel_id=1, source_target_pairs={{0,1},{1,0},{2,3},{3,2},{4,5},{5,4},{6,7},{7,6},{8,9},{9,8},{10,11... | collective-permute-start | bytes 2654216 | tf_op jit(solution)/shard_map/ppermute | solution.py:34
  162.1 15.2 %collective-permute-start.24 = (bf16[384,768]{1,0:T(8,128)(2,1)S(1)}, bf16[384,768]{1,0:T(8,128)(2,1)S(1)}, u32[]{:S(2)}, u32[]{:S(2)}) collective-permute-start(bf16[384,768]{1,0:T(8,128)(2,1)S(1)} %constant_dynamic-slice_fusion.6), channel_id=1, source_target_pairs={{0,8},{8,0},{16,24},{24,16},{1,9},{9,1},{17,25},{25,17},{2,10},{10... | collective-permute-start | bytes 1769480 | tf_op jit(solution)/shard_map/ppermute | solution.py:1191
  182.4 31.8 %collective-permute-start.30 = (bf16[192,2048]{1,0:T(8,128)(2,1)}, bf16[192,2048]{1,0:T(8,128)(2,1)}, u32[]{:S(2)}, u32[]{:S(2)}) collective-permute-start(bf16[192,2048]{1,0:T(8,128)(2,1)} %dynamic-slice_bitcast_fusion), channel_id=1, source_target_pairs={{0,1},{1,0},{2,3},{3,2},{4,5},{5,4},{6,7},{7,6},{8,9},{9,8},{10,11... | collective-permute-start | bytes 2359304 | tf_op jit(solution)/shard_map/ppermute | solution.py:34
  187.7 26.5 %collective-permute-start.28 = (bf16[1024,384]{1,0:T(8,128)(2,1)}, bf16[1024,384]{1,0:T(8,128)(2,1)}, u32[]{:S(2)}, u32[]{:S(2)}) collective-permute-start(bf16[1024,384]{1,0:T(8,128)(2,1)} %add_convert_fusion.2), channel_id=1, source_target_pairs={{0,4},{4,0},{1,5},{5,1},{2,6},{6,2},{3,7},{7,3},{8,12},{12,8},{9,1... | collective-permute-start | bytes 2359304 | tf_op jit(solution)/shard_map/ppermute | solution.py:34
  190.4 23.9 %collective-permute-start.29 = (bf16[192,768]{1,0:T(8,128)(2,1)}, bf16[192,768]{1,0:T(8,128)(2,1)}, u32[]{:S(2)}, u32[]{:S(2)}) collective-permute-start(bf16[192,768]{1,0:T(8,128)(2,1)} %constant_dynamic-slice_fusion.5), channel_id=1, source_target_pairs={{0,16},{16,0},{8,24},{24,8},{1,17},{17,1},{9,25},{25,9},{2,18},{18... | collective-permute-start | bytes 884744 | tf_op jit(solution)/shard_map/ppermute | solution.py:1194
  191.7 21.2 %collective-permute-start.32 = (bf16[192,256]{1,0:T(8,128)(2,1)S(1)}, bf16[192,256]{1,0:T(8,128)(2,1)S(1)}, u32[]{:S(2)}, u32[]{:S(2)}) collective-permute-start(bf16[192,256]{1,0:T(8,128)(2,1)S(1)} %copy-done.22), channel_id=1, source_target_pairs={{0,16},{16,0},{8,24},{24,8},{1,17},{17,1},{9,25},{25,9},{2,18},{18... | collective-permute-start | bytes 294920 | tf_op jit(solution)/shard_map/ppermute | solution.py:1069
  198.6 15.0 %collective-permute-start.33 = (bf16[192,256]{1,0:T(8,128)(2,1)S(1)}, bf16[192,256]{1,0:T(8,128)(2,1)S(1)}, u32[]{:S(2)}, u32[]{:S(2)}) collective-permute-start(bf16[192,256]{1,0:T(8,128)(2,1)S(1)} %copy-done.25), channel_id=1, source_target_pairs={{0,24},{24,0},{8,16},{16,8},{1,25},{25,1},{9,17},{17,9},{2,26},{26... | collective-permute-start | bytes 294920 | tf_op jit(solution)/shard_map/ppermute | solution.py:1069
  222.6 16.1 %collective-permute-start.36 = (bf16[96,2048]{1,0:T(8,128)(2,1)}, bf16[96,2048]{1,0:T(8,128)(2,1)}, u32[]{:S(2)}, u32[]{:S(2)}) collective-permute-start(bf16[96,2048]{1,0:T(8,128)(2,1)} %constant_dynamic-slice_fusion.4), channel_id=1, source_target_pairs={{0,8},{8,0},{16,24},{24,16},{1,9},{9,1},{17,25},{25,17},{2,10},{10... | collective-permute-start | bytes 1179656 | tf_op jit(solution)/shard_map/ppermute | solution.py:1191
  227.2 20.0 %collective-permute-start.38 = (bf16[384,256]{1,0:T(8,128)(2,1)}, bf16[384,256]{1,0:T(8,128)(2,1)S(1)}, u32[]{:S(2)}, u32[]{:S(2)}) collective-permute-start(bf16[384,256]{1,0:T(8,128)(2,1)} %copy-done.35), channel_id=1, source_target_pairs={{0,8},{8,0},{16,24},{24,16},{1,9},{9,1},{17,25},{25,17},{2,10},{10... | collective-permute-start | bytes 589832 | tf_op jit(solution)/shard_map/ppermute | solution.py:1069
  227.2 23.1 %collective-permute-start.39 = (bf16[384,256]{1,0:T(8,128)(2,1)}, bf16[384,256]{1,0:T(8,128)(2,1)S(1)}, u32[]{:S(2)}, u32[]{:S(2)}) collective-permute-start(bf16[384,256]{1,0:T(8,128)(2,1)} %copy-done.33), channel_id=1, source_target_pairs={{0,16},{16,0},{8,24},{24,8},{1,17},{17,1},{9,25},{25,9},{2,18},{18... | collective-permute-start | bytes 589832 | tf_op jit(solution)/shard_map/ppermute | solution.py:1069
  231.4 20.1 %collective-permute-start.40 = (bf16[384,256]{1,0:T(8,128)(2,1)}, bf16[384,256]{1,0:T(8,128)(2,1)S(1)}, u32[]{:S(2)}, u32[]{:S(2)}) collective-permute-start(bf16[384,256]{1,0:T(8,128)(2,1)} %copy-done.31), channel_id=1, source_target_pairs={{0,24},{24,0},{8,16},{16,8},{1,25},{25,1},{9,17},{17,9},{2,26},{26... | collective-permute-start | bytes 589832 | tf_op jit(solution)/shard_map/ppermute | solution.py:1069
  233.4 28.1 %collective-permute-start.42 = (bf16[96,768]{1,0:T(8,128)(2,1)S(1)}, bf16[96,768]{1,0:T(8,128)(2,1)S(1)}, u32[]{:S(2)}, u32[]{:S(2)}) collective-permute-start(bf16[96,768]{1,0:T(8,128)(2,1)S(1)} %add_convert_fusion.9), channel_id=1, source_target_pairs={{0,16},{16,0},{8,24},{24,8},{1,17},{17,1},{9,25},{25,9},{2,18},{18... | collective-permute-start | bytes 442376 | tf_op jit(solution)/shard_map/ppermute | solution.py:1194
  245.0 16.5 %collective-permute-start.41 = (bf16[48,2048]{1,0:T(8,128)(2,1)S(1)}, bf16[48,2048]{1,0:T(8,128)(2,1)S(1)}, u32[]{:S(2)}, u32[]{:S(2)}) collective-permute-start(bf16[48,2048]{1,0:T(8,128)(2,1)S(1)} %constant_dynamic-slice_fusion.2), channel_id=1, source_target_pairs={{0,16},{16,0},{8,24},{24,8},{1,17},{17,1},{9,25},{25,9},{2,18},{18... | collective-permute-start | bytes 589832 | tf_op jit(solution)/shard_map/ppermute | solution.py:1194
  247.2 36.5 %collective-permute-start.49 = (bf16[576,768]{1,0:T(8,128)(2,1)S(1)}, bf16[576,768]{1,0:T(8,128)(2,1)S(1)}, u32[]{:S(2)}, u32[]{:S(2)}) collective-permute-start(bf16[576,768]{1,0:T(8,128)(2,1)S(1)} %copy-done.29), channel_id=1, source_target_pairs={{0,2},{2,0},{1,3},{3,1},{4,6},{6,4},{5,7},{7,5},{8,10},{10,8},{9,1... | collective-permute-start | bytes 2654216 | tf_op jit(solution)/shard_map/ppermute | solution.py:34
  263.2 20.0 %collective-permute-start.46 = (bf16[208,640]{1,0:T(8,128)(2,1)S(1)}, bf16[208,640]{1,0:T(8,128)(2,1)S(1)}, u32[]{:S(2)}, u32[]{:S(2)}) collective-permute-start(bf16[208,640]{1,0:T(8,128)(2,1)S(1)} %add_convert_fusion.6), channel_id=1, source_target_pairs={{0,16},{16,0},{8,24},{24,8},{1,17},{17,1},{9,25},{25,9},{2,18},{18... | collective-permute-start | bytes 798728 | tf_op jit(solution)/shard_map/ppermute | solution.py:1194
  274.6 23.3 %collective-permute-start.48 = (bf16[384,768]{1,0:T(8,128)(2,1)S(1)}, bf16[384,768]{1,0:T(8,128)(2,1)S(1)}, u32[]{:S(2)}, u32[]{:S(2)}) collective-permute-start(bf16[384,768]{1,0:T(8,128)(2,1)S(1)} %bitcast.47), channel_id=1, source_target_pairs={{0,4},{4,0},{1,5},{5,1},{2,6},{6,2},{3,7},{7,3},{8,12},{12,8},{9,1... | collective-permute-start | bytes 1769480 | tf_op jit(solution)/shard_map/ppermute | solution.py:34
  283.4 14.6 %collective-permute-start.50 = (bf16[416,640]{1,0:T(8,128)(2,1)S(1)}, bf16[416,640]{1,0:T(8,128)(2,1)S(1)}, u32[]{:S(2)}, u32[]{:S(2)}) collective-permute-start(bf16[416,640]{1,0:T(8,128)(2,1)S(1)} %maximum_select_fusion.3), channel_id=1, source_target_pairs={{0,8},{8,0},{16,24},{24,16},{1,9},{9,1},{17,25},{25,17},{2,10},{10... | collective-permute-start | bytes 1597448 | tf_op jit(solution)/shard_map/ppermute | solution.py:1191
  283.6 21.2 %collective-permute-start.51 = (bf16[192,2048]{1,0:T(8,128)(2,1)S(1)}, bf16[192,2048]{1,0:T(8,128)(2,1)}, u32[]{:S(2)}, u32[]{:S(2)}) collective-permute-start(bf16[192,2048]{1,0:T(8,128)(2,1)S(1)} %maximum_select_fusion.1.refs_0_), channel_id=1, source_target_pairs={{0,4},{4,0},{1,5},{5,1},{2,6},{6,2},{3,7},{7,3},{8,12},{12,8},{9,1... | collective-permute-start | bytes 2359304 | tf_op jit(solution)/shard_map/ppermute | solution.py:34
  287.6 14.2 %collective-permute-start.52 = (bf16[384,768]{1,0:T(8,128)(2,1)S(1)}, bf16[384,768]{1,0:T(8,128)(2,1)S(1)}, u32[]{:S(2)}, u32[]{:S(2)}) collective-permute-start(bf16[384,768]{1,0:T(8,128)(2,1)S(1)} %bitcast.48), channel_id=1, source_target_pairs={{0,2},{2,0},{1,3},{3,1},{4,6},{6,4},{5,7},{7,5},{8,10},{10,8},{9,1... | collective-permute-start | bytes 1769480 | tf_op jit(solution)/shard_map/ppermute | solution.py:34
  (103 other events, 845.9 us)

commit v2 on v1

--- a/solution.py
+++ b/solution.py
@@ -1223,15 +1223,15 @@
         head_weights = [*low_heads, head_got, swap(head_got, "c")]
         pair_got = swap(pairs[1], "c")
         query_got = exchange(query_low)
-        down_sum = add_pair(part_of(down_sum, near_bit, 2, 0), down_got)
-        down_got = to_far(part_of(down_sum, 1 - far_bit, 2, 0))
         up_sum = add_pair(up_kept, up_got).reshape(2, own_rows // 2, -1)
         up_got = swap(lax.dynamic_index_in_dim(up_sum, 1 - w_at, 0, keepdims=False), "w")
         pair_got = arrive(pair_got)
         half_rows = pair_got.shape[0] // 2
         pair_sent = add_pair(pairs[0][half_rows:], pair_got[half_rows:])
-        pair_sent = arrive(pair_sent)
+        pair_sent, down_got = arrive(pair_sent, down_got)
         key_got = swap(pair_sent, "x")
+        down_sum = add_pair(part_of(down_sum, near_bit, 2, 0), down_got)
+        down_got = to_far(part_of(down_sum, 1 - far_bit, 2, 0))
         key_got, down_got, up_got, *query_got = arrive(key_got, down_got, up_got, *query_got)
         up_sum = add_pair(lax.dynamic_index_in_dim(up_sum, w_at, 0, keepdims=False), up_got)
         up_sent, key_got = arrive(part_of(up_sum, 1 - near_bit, 2, 0), key_got)

time: 320 us -> 320 us (level)
  Pallas kernels: 99.4 us -> 126 us
  waiting for transfers between devices: 84.4 us -> 64.2 us
  starting transfers between devices: 91.3 us -> 84.5 us
    ppermute x32, waiting for transfers between devices: 33.6 us -> 14.9 us  [swap(): return lax.ppermute(value, axis, SWAP)]
    pallas_call x2, Pallas kernels: 24.9 us -> 41 us  [attend_backward(): pl.pallas_call(partial(backward_kernel, blocks=blocks, rows=2 * half_rows...]
    pallas_call x1, Pallas kernels: 15 us -> 25.8 us  [attend_forward(): pl.pallas_call(partial(forward_kernel, blocks=blocks, rows=2 * half_rows...]
    ppermute x32, starting transfers between devices: 61.9 us -> 55.3 us  [swap(): return lax.ppermute(value, axis, SWAP)]
  transfers between devices with their start and end apart: 57 -> 57, of which waited for: 18 -> 15; matrix products, arithmetic and copies ran while one was open for 5% -> 5% of each run, Pallas kernels for 23% -> 32%
where the time goes in v2:
time: 320 us
  Pallas kernels  126 us (39%)
  starting transfers between devices  84.5 us (26%)
  waiting for transfers between devices  64.2 us (20%)
  local copies, waits for them, and re-layouts  27.9 us (9%)
  other arithmetic  14.5 us (5%)
    ppermute x32, starting transfers between devices, swap(): return lax.ppermute(value, axis, SWAP)  55.3 us
    pallas_call x2, Pallas kernels, attend_backward(): pl.pallas_call(partial(backward_kernel, blocks=blocks, rows=2 * half_rows...  41 us
    pallas_call x1, Pallas kernels, attend_forward(): pl.pallas_call(partial(forward_kernel, blocks=blocks, rows=2 * half_rows...  25.8 us
    ppermute x5, waiting for transfers between devices, to_far(): return lax.ppermute(value, 'z', far)  25 us
    unnamed x156, local copies, waits for them, and re-layouts  20.2 us
    ppermute x12, waiting for transfers between devices, exchange(): lax.ppermute(item, 'z', perm)  18.2 us
    pallas_call x1, Pallas kernels, middle(): pl.pallas_call(partial(middle_kernel, groups=groups, shared=len(weights)...  15.9 us
    ppermute x32, waiting for transfers between devices, swap(): return lax.ppermute(value, axis, SWAP)  14.9 us
  transfers between devices with their start and end apart: 57, of which 15 were waited for; matrix products, arithmetic and copies ran while one was open for 5% of the time, Pallas kernels for 32%

profile of v2, /device:TPU:1, one launch (start us, length us, event | category | flops | bytes accessed | tf_op | source)
XLA Modules:
  0.0 319.9 jit_solution(9741281359275802915)
XLA Ops:
  4.0 2.3 collective-permute-start.4
  6.9 4.6 %prepare.1 = (bf16[384,384]{1,0:T(8,128)(2,1)}, bf16[384,192]{1,0:T(8,128)(2,1)}, bf16[384,768]{1,0:T(8,128)(2,1)}, bf16[384,768]{1,0:T(8,128)(2,1)}, bf16[384,7...) custom-call(s32[2]{0:T(128)} %get-tuple-element.344.meta_ref, f32[384,768]{1,0:T(8,128)} %refs_0_.1, f32[384,768]{1,0:T(8,128)} %refs_1_.1, ...), custom_call_target="tpu_custom_call" | custom-call | flops 1000 | bytes 1 | tf_op jit(solution)/shard_map/prepare/pallas_call | solution.py:366
  14.5 8.3 %round_weights.1 = (bf16[384,768]{1,0:T(8,128)(2,1)}, bf16[384,3072]{1,0:T(8,128)(2,1)}, bf16[1536,768]{1,0:T(8,128)(2,1)}, bf16[1728,768]{1,0:T(8,128)(2,1)}) custom-call(s32[2]{0:T(128)} %get-tuple-element.344.meta_ref, f32[384,768]{1,0:T(8,128)} %out_w.1, f32[384,3072]{1,0:T(8,128)} %up_w.1, f32[1536,768]{1,0:T(8,128)} %down_w.1), custom_call_target="tpu_custom_call" | custom-call | flops 1000 | bytes 1 | tf_op jit(solution)/shard_map/round_weights/pallas_call | solution.py:264
  28.0 4.9 %collective-permute-done.5.second_ref = bf16[256,768]{1,0:T(8,128)(2,1)S(1)} collective-permute-done((bf16[256,768]{1,0:T(8,128)(2,1)S(1)}, bf16[256,768]{1,0:T(8,128)(2,1)S(1)}, u32[]{:S(2)}, u32[]{:S(2)}) %collective-permute-start.5) | collective-permute-done | bytes 393248 | tf_op jit(solution)/shard_map/ppermute | solution.py:1122
  37.5 3.8 %collective-permute-start.9 = (bf16[512,384]{1,0:T(8,128)(2,1)S(1)}, bf16[512,384]{1,0:T(8,128)(2,1)S(1)}, u32[]{:S(2)}, u32[]{:S(2)}) collective-permute-start(bf16[512,384]{1,0:T(8,128)(2,1)S(1)} %get-tuple-element.190.refs_3_.refs_9_), channel_id=1, source_target_pairs={{0,2},{2,0},{1,3},{3,1},{4,6},{6,4},{5,7},{7,5},{8,10},{10,8},{9,1... | collective-permute-start | bytes 1179656 | tf_op jit(solution)/shard_map/ppermute | solution.py:34
  43.5 7.9 %collective-permute-start.11 = (bf16[512,384]{1,0:T(8,128)(2,1)S(1)}, bf16[512,384]{1,0:T(8,128)(2,1)S(1)}, u32[]{:S(2)}, u32[]{:S(2)}) collective-permute-start(bf16[512,384]{1,0:T(8,128)(2,1)S(1)} %collective-permute-done.7.refs_5_.refs_11_), channel_id=1, source_target_pairs={{0,2},{2,0},{1,3},{3,1},{4,6},{6,4},{5,7},{7,5},{8,10},{10,8},{9,1... | collective-permute-start | bytes 1179656 | tf_op jit(solution)/shard_map/ppermute | solution.py:34
  51.9 4.1 %collective-permute-start.10 = (bf16[512,384]{1,0:T(8,128)(2,1)S(1)}, bf16[512,384]{1,0:T(8,128)(2,1)S(1)}, u32[]{:S(2)}, u32[]{:S(2)}) collective-permute-start(bf16[512,384]{1,0:T(8,128)(2,1)S(1)} %collective-permute-done.6.refs_4_.refs_10_), channel_id=1, source_target_pairs={{0,2},{2,0},{1,3},{3,1},{4,6},{6,4},{5,7},{7,5},{8,10},{10,8},{9,1... | collective-permute-start | bytes 1179656 | tf_op jit(solution)/shard_map/ppermute | solution.py:34
  58.7 25.8 %attend_forward.1 = (f32[192,1024]{1,0:T(8,128)}, bf16[192,256]{1,0:T(8,128)(2,1)}, bf16[192,256]{1,0:T(8,128)(2,1)}, bf16[192,256]{1,0:T(8,128)(2,1)}, bf16[192,256]{1,0:T(8,128)(2,1)}, /*index=5*/f32[3,1,1024]{2,1,0:T(1,128)}) custom-call(s32[6]{0:T(128)} %stack.99.meta_ref, bf16[192,512]{1,0:T(8,128)(2,1)} %copy-done.15, bf16[192,512]{1,0:T(8,128)(2,1)} %copy-done.16, ...), custom_call_target="tpu_custom_call" | custom-call | flops 24000 | bytes 1 | tf_op jit(solution)/shard_map/attend_forward/pallas_call | solution.py:125
  85.4 3.4 %collective-permute-start.16 = (bf16[192,256]{1,0:T(8,128)(2,1)}, bf16[192,256]{1,0:T(8,128)(2,1)S(1)}, u32[]{:S(2)}, u32[]{:S(2)}) collective-permute-start(bf16[192,256]{1,0:T(8,128)(2,1)} %get-tuple-element.198), channel_id=1, source_target_pairs={{0,24},{24,0},{8,16},{16,8},{1,25},{25,1},{9,17},{17,9},{2,26},{26... | collective-permute-start | bytes 294920 | tf_op jit(solution)/shard_map/ppermute | solution.py:1069
  93.7 15.9 %middle.1 = (f32[256,768]{1,0:T(8,128)}, f32[256,768]{1,0:T(8,128)}, bf16[192,256]{1,0:T(8,128)(2,1)}, bf16[192,256]{1,0:T(8,128)(2,1)}, bf16[192,256]{1,0:T(8,1...) custom-call(s32[4]{0:T(128)} %pad_add_fusion.2.meta_ref, ...), custom_call_target="tpu_custom_call" | custom-call | flops 15000 | bytes 1 | tf_op jit(solution)/shard_map/middle/pallas_call | solution.py:641
  109.6 4.1 %collective-permute-start.18 = (bf16[6144,256]{1,0:T(8,128)(2,1)}, bf16[6144,256]{1,0:T(8,128)(2,1)S(1)}, u32[]{:S(2)}, u32[]{:S(2)}) collective-permute-start(bf16[6144,256]{1,0:T(8,128)(2,1)} %get-tuple-element.205.own_ffn_ref.send_ref), channel_id=1, source_target_pairs={{0,2},{2,0},{1,3},{3,1},{4,6},{6,4},{5,7},{7,5},{8,10},{10,8},{9,1... | collective-permute-start | bytes 9437192 | tf_op jit(solution)/shard_map/ppermute | solution.py:34
  124.9 2.3 down_slab.2
  127.7 2.9 up_slabs.1
  134.7 26.5 %attend_backward.2 = (bf16[192,256]{1,0:T(8,128)(2,1)}, bf16[192,256]{1,0:T(8,128)(2,1)}, bf16[192,256]{1,0:T(8,128)(2,1)}, bf16[192,256]{1,0:T(8,128)(2,1)}, bf...) custom-call(s32[6]{0:T(128)} %stack.99.meta_ref, bf16[192,512]{1,0:T(8,128)(2,1)} %copy-done.15, ...), custom_call_target="tpu_custom_call" | custom-call | flops 24000 | bytes 1 | tf_op jit(solution)/shard_map/attend_backward/pallas_call | solution.py:226
  166.1 14.6 %attend_backward.3 = (bf16[192,256]{1,0:T(8,128)(2,1)}, bf16[192,256]{1,0:T(8,128)(2,1)}, bf16[192,256]{1,0:T(8,128)(2,1)}, bf16[192,256]{1,0:T(8,128)(2,1)}, bf...) custom-call(s32[6]{0:T(128)} %stack.99.meta_ref, ...), custom_call_target="tpu_custom_call", output_to_operand_aliasing={{0}: (17, {}), {1}: (18, {}), {2}: (19, {}), {3}: (20, {}),... | custom-call | flops 12000 | bytes 1 | tf_op jit(solution)/shard_map/attend_backward/pallas_call | solution.py:226
  193.9 6.0 %collective-permute-done.31.refs_1_ = bf16[192,256]{1,0:T(8,128)(2,1)S(1)} collective-permute-done((bf16[192,256]{1,0:T(8,128)(2,1)S(1)}, bf16[192,256]{1,0:T(8,128)(2,1)S(1)}, u32[]{:S(2)}, u32[]{:S(2)}) %collective-permute-start.31) | collective-permute-done | bytes 98336 | tf_op jit(solution)/shard_map/ppermute | solution.py:1069
  202.1 11.8 %collective-permute-done.32.refs_2_ = bf16[192,256]{1,0:T(8,128)(2,1)S(1)} collective-permute-done((bf16[192,256]{1,0:T(8,128)(2,1)S(1)}, bf16[192,256]{1,0:T(8,128)(2,1)S(1)}, u32[]{:S(2)}, u32[]{:S(2)}) %collective-permute-start.32) | collective-permute-done | bytes 98336 | tf_op jit(solution)/shard_map/ppermute | solution.py:1069
  220.4 2.5 head_slab.2
  229.4 2.9 collective-permute-done.34
  241.3 4.8 %collective-permute-done.37 = bf16[208,640]{1,0:T(8,128)(2,1)S(1)} collective-permute-done((bf16[208,640]{1,0:T(8,128)(2,1)S(1)}, bf16[208,640]{1,0:T(8,128)(2,1)S(1)}, u32[]{:S(2)}, u32[]{:S(2)}) %collective-permute-start.37) | collective-permute-done | bytes 266272 | tf_op jit(solution)/shard_map/ppermute | solution.py:34
  248.2 3.0 collective-permute-start.49
  252.4 10.1 %collective-permute-done.41 = bf16[48,2048]{1,0:T(8,128)(2,1)S(1)} collective-permute-done((bf16[48,2048]{1,0:T(8,128)(2,1)S(1)}, bf16[48,2048]{1,0:T(8,128)(2,1)S(1)}, u32[]{:S(2)}, u32[]{:S(2)}) %collective-permute-start.41) | collective-permute-done | bytes 196640 | tf_op jit(solution)/shard_map/ppermute | solution.py:1194
  265.3 6.6 %collective-permute-done.44 = bf16[48,2048]{1,0:T(8,128)(2,1)S(1)} collective-permute-done((bf16[48,2048]{1,0:T(8,128)(2,1)S(1)}, bf16[48,2048]{1,0:T(8,128)(2,1)S(1)}, u32[]{:S(2)}, u32[]{:S(2)}) %collective-permute-start.44) | collective-permute-done | bytes 196640 | tf_op jit(solution)/shard_map/ppermute | solution.py:1194
  272.0 2.4 collective-permute-start.47
  276.0 8.3 %collective-permute-done.46 = bf16[208,640]{1,0:T(8,128)(2,1)S(1)} collective-permute-done((bf16[208,640]{1,0:T(8,128)(2,1)S(1)}, bf16[208,640]{1,0:T(8,128)(2,1)S(1)}, u32[]{:S(2)}, u32[]{:S(2)}) %collective-permute-start.46) | collective-permute-done | bytes 266272 | tf_op jit(solution)/shard_map/ppermute | solution.py:1194
  284.8 3.8 %token_gradient.1 = f32[256,768]{1,0:T(8,128)} custom-call(s32[4]{0:T(128)S(1)} %copy-done.48, f32[256,768]{1,0:T(8,128)S(1)} %copy-done.30, bf16[192,256]{1,0:T(8,128)(2,1)S(1)} %copy-done.17, bf16[192,256]{1,0:T(8,128)(2,1)S(1)} %copy-done.42, bf16[192,256]{1,0:T(8,128)(2,1)S(1)} %copy-done.44, bf16[192,256]{1,0:T(8,128)(2,1)S(1)} %copy-done.46, ...), custom_call_target="tpu_custom_call" | custom-call | flops 4000 | bytes 1 | tf_op jit(solution)/shard_map/token_gradient/pallas_call | solution.py:889
  288.6 10.2 %collective-permute-start.52 = (bf16[384,768]{1,0:T(8,128)(2,1)S(1)}, bf16[384,768]{1,0:T(8,128)(2,1)S(1)}, u32[]{:S(2)}, u32[]{:S(2)}) collective-permute-start(bf16[384,768]{1,0:T(8,128)(2,1)S(1)} %bitcast.48), channel_id=1, source_target_pairs={{0,2},{2,0},{1,3},{3,1},{4,6},{6,4},{5,7},{7,5},{8,10},{10,8},{9,1... | collective-permute-start | bytes 1769480 | tf_op jit(solution)/shard_map/ppermute | solution.py:34
  299.3 3.4 %collective-permute-start.54 = (bf16[832,640]{1,0:T(8,128)(2,1)S(1)}, bf16[832,640]{1,0:T(8,128)(2,1)S(1)}, u32[]{:S(2)}, u32[]{:S(2)}) collective-permute-start(bf16[832,640]{1,0:T(8,128)(2,1)S(1)} %maximum_select_fusion.own_ref), channel_id=1, source_target_pairs={{0,2},{2,0},{1,3},{3,1},{4,6},{6,4},{5,7},{7,5},{8,10},{10,8},{9,1... | collective-permute-start | bytes 3194888 | tf_op jit(solution)/shard_map/ppermute | solution.py:34
  302.8 3.0 down_finish.1
  305.8 3.8 %collective-permute-start.56 = (bf16[192,2048]{1,0:T(8,128)(2,1)}, bf16[192,2048]{1,0:T(8,128)(2,1)}, u32[]{:S(2)}, u32[]{:S(2)}) collective-permute-start(bf16[192,2048]{1,0:T(8,128)(2,1)} %collective-permute-done.51.refs_1_), channel_id=1, source_target_pairs={{0,2},{2,0},{1,3},{3,1},{4,6},{6,4},{5,7},{7,5},{8,10},{10,8},{9,1... | collective-permute-start | bytes 2359304 | tf_op jit(solution)/shard_map/ppermute | solution.py:34
  309.6 2.7 head_finish.1
  313.6 5.1 %up_finish.1 = (f32[384,3072]{1,0:T(8,128)}, f32[384,768]{1,0:T(8,128)}, f32[384,128]{1,0:T(8,128)S(1)}) custom-call(s32[2]{0:T(128)S(1)} %pad_add_fusion.5.meta_ref, bf16[192,2048]{1,0:T(8,128)(2,1)S(1)} %maximum_select_fusion.1.refs_0_, bf16[192,2048]{1,0:T(8,128)(2,1)} %collective-permute-done.51.refs_1_, ...), custom_call_target="tpu_custom_call" | custom-call | flops 5000 | bytes 1 | tf_op jit(solution)/shard_map/up_finish/pallas_call | solution.py:959
  (317 shorter events, 95.8 us)
Async XLA Ops:
  1.8 21.5 %collective-permute-start.3 = (bf16[256,768]{1,0:T(8,128)(2,1)S(1)}, bf16[256,768]{1,0:T(8,128)(2,1)S(1)}, u32[]{:S(2)}, u32[]{:S(2)}) collective-permute-start(bf16[256,768]{1,0:T(8,128)(2,1)S(1)} %bitcast_convert_fusion.first_ref), channel_id=1, source_target_pairs={{0,8},{8,0},{16,24},{24,16},{1,9},{9,1},{17,25},{25,17},{2,10},{10... | collective-permute-start | bytes 1179656 | tf_op jit(solution)/shard_map/ppermute | solution.py:1079
  4.0 19.3 %collective-permute-start.4 = (bf16[256,768]{1,0:T(8,128)(2,1)S(1)}, bf16[256,768]{1,0:T(8,128)(2,1)S(1)}, u32[]{:S(2)}, u32[]{:S(2)}) collective-permute-start(bf16[256,768]{1,0:T(8,128)(2,1)S(1)} %bitcast_convert_fusion.first_ref), channel_id=1, source_target_pairs={{0,16},{16,0},{8,24},{24,8},{1,17},{17,1},{9,25},{25,9},{2,18},{18... | collective-permute-start | bytes 1179656 | tf_op jit(solution)/shard_map/ppermute | solution.py:1080
  23.4 61.2 %collective-permute-start.12 = (bf16[1728,768]{1,0:T(8,128)(2,1)}, bf16[1728,768]{1,0:T(8,128)(2,1)}, u32[]{:S(2)}, u32[]{:S(2)}) collective-permute-start(bf16[1728,768]{1,0:T(8,128)(2,1)} %get-tuple-element.192), channel_id=1, source_target_pairs={{0,1},{1,0},{2,3},{3,2},{4,5},{5,4},{6,7},{7,6},{8,9},{9,8},{10,11... | collective-permute-start | bytes 7962632 | tf_op jit(solution)/shard_map/ppermute | solution.py:34
  37.3 14.6 %collective-permute-start.6 = (bf16[512,384]{1,0:T(8,128)(2,1)S(1)}, bf16[512,384]{1,0:T(8,128)(2,1)S(1)}, u32[]{:S(2)}, u32[]{:S(2)}) collective-permute-start(bf16[512,384]{1,0:T(8,128)(2,1)S(1)} %get-tuple-element.189.refs_2_.refs_8_), channel_id=1, source_target_pairs={{0,4},{4,0},{1,5},{5,1},{2,6},{6,2},{3,7},{7,3},{8,12},{12,8},{9,1... | collective-permute-start | bytes 1179656 | tf_op jit(solution)/shard_map/ppermute | solution.py:34
  37.5 20.0 %collective-permute-start.9 = (bf16[512,384]{1,0:T(8,128)(2,1)S(1)}, bf16[512,384]{1,0:T(8,128)(2,1)S(1)}, u32[]{:S(2)}, u32[]{:S(2)}) collective-permute-start(bf16[512,384]{1,0:T(8,128)(2,1)S(1)} %get-tuple-element.190.refs_3_.refs_9_), channel_id=1, source_target_pairs={{0,2},{2,0},{1,3},{3,1},{4,6},{6,4},{5,7},{7,5},{8,10},{10,8},{9,1... | collective-permute-start | bytes 1179656 | tf_op jit(solution)/shard_map/ppermute | solution.py:34
  41.4 16.2 %collective-permute-start.8 = (bf16[512,384]{1,0:T(8,128)(2,1)S(1)}, bf16[512,384]{1,0:T(8,128)(2,1)S(1)}, u32[]{:S(2)}, u32[]{:S(2)}) collective-permute-start(bf16[512,384]{1,0:T(8,128)(2,1)S(1)} %get-tuple-element.189.refs_2_.refs_8_), channel_id=1, source_target_pairs={{0,2},{2,0},{1,3},{3,1},{4,6},{6,4},{5,7},{7,5},{8,10},{10,8},{9,1... | collective-permute-start | bytes 1179656 | tf_op jit(solution)/shard_map/ppermute | solution.py:34
  43.5 14.1 %collective-permute-start.11 = (bf16[512,384]{1,0:T(8,128)(2,1)S(1)}, bf16[512,384]{1,0:T(8,128)(2,1)S(1)}, u32[]{:S(2)}, u32[]{:S(2)}) collective-permute-start(bf16[512,384]{1,0:T(8,128)(2,1)S(1)} %collective-permute-done.7.refs_5_.refs_11_), channel_id=1, source_target_pairs={{0,2},{2,0},{1,3},{3,1},{4,6},{6,4},{5,7},{7,5},{8,10},{10,8},{9,1... | collective-permute-start | bytes 1179656 | tf_op jit(solution)/shard_map/ppermute | solution.py:34
  113.7 13.6 %collective-permute-start.19 = (f32[16,768]{1,0:T(8,128)}, f32[16,768]{1,0:T(8,128)S(1)}, u32[]{:S(2)}, u32[]{:S(2)}) collective-permute-start(f32[16,768]{1,0:T(8,128)} %get-tuple-element.206.own_small_ref), channel_id=1, source_target_pairs={{0,2},{2,0},{1,3},{3,1},{4,6},{6,4},{5,7},{7,5},{8,10},{10,8},{9,1... | collective-permute-start | bytes 147464 | tf_op jit(solution)/shard_map/ppermute | solution.py:34
  113.8 18.0 %collective-permute-start.20 = (bf16[192,256]{1,0:T(8,128)(2,1)}, bf16[192,256]{1,0:T(8,128)(2,1)S(1)}, u32[]{:S(2)}, u32[]{:S(2)}) collective-permute-start(bf16[192,256]{1,0:T(8,128)(2,1)} %get-tuple-element.209), channel_id=1, source_target_pairs={{0,8},{8,0},{16,24},{24,16},{1,9},{9,1},{17,25},{25,17},{2,10},{10... | collective-permute-start | bytes 294920 | tf_op jit(solution)/shard_map/ppermute | solution.py:1069
  115.0 16.8 %collective-permute-start.21 = (bf16[192,256]{1,0:T(8,128)(2,1)}, bf16[192,256]{1,0:T(8,128)(2,1)S(1)}, u32[]{:S(2)}, u32[]{:S(2)}) collective-permute-start(bf16[192,256]{1,0:T(8,128)(2,1)} %get-tuple-element.210), channel_id=1, source_target_pairs={{0,16},{16,0},{8,24},{24,8},{1,17},{17,1},{9,25},{25,9},{2,18},{18... | collective-permute-start | bytes 294920 | tf_op jit(solution)/shard_map/ppermute | solution.py:1069
  115.1 16.7 %collective-permute-start.22 = (bf16[192,256]{1,0:T(8,128)(2,1)}, bf16[192,256]{1,0:T(8,128)(2,1)S(1)}, u32[]{:S(2)}, u32[]{:S(2)}) collective-permute-start(bf16[192,256]{1,0:T(8,128)(2,1)} %get-tuple-element.211), channel_id=1, source_target_pairs={{0,24},{24,0},{8,16},{16,8},{1,25},{25,1},{9,17},{17,9},{2,26},{26... | collective-permute-start | bytes 294920 | tf_op jit(solution)/shard_map/ppermute | solution.py:1069
  131.8 29.3 %collective-permute-start.23 = (bf16[768,768]{1,0:T(8,128)(2,1)}, bf16[768,768]{1,0:T(8,128)(2,1)S(1)}, u32[]{:S(2)}, u32[]{:S(2)}) collective-permute-start(bf16[768,768]{1,0:T(8,128)(2,1)} %down_slab.2), channel_id=1, source_target_pairs={{0,1},{1,0},{2,3},{3,2},{4,5},{5,4},{6,7},{7,6},{8,9},{9,8},{10,11... | collective-permute-start | bytes 3538952 | tf_op jit(solution)/shard_map/ppermute | solution.py:34
  132.2 48.5 %collective-permute-start.25 = (bf16[384,2048]{1,0:T(8,128)(2,1)}, bf16[384,2048]{1,0:T(8,128)(2,1)}, u32[]{:S(2)}, u32[]{:S(2)}) collective-permute-start(bf16[384,2048]{1,0:T(8,128)(2,1)} %get-tuple-element.229), channel_id=1, source_target_pairs={{0,4},{4,0},{1,5},{5,1},{2,6},{6,2},{3,7},{7,3},{8,12},{12,8},{9,1... | collective-permute-start | bytes 4718600 | tf_op jit(solution)/shard_map/ppermute | solution.py:34
  133.5 47.2 %collective-permute-start.26 = (bf16[576,768]{1,0:T(8,128)(2,1)}, bf16[576,768]{1,0:T(8,128)(2,1)S(1)}, u32[]{:S(2)}, u32[]{:S(2)}) collective-permute-start(bf16[576,768]{1,0:T(8,128)(2,1)} %get-tuple-element.230), channel_id=1, source_target_pairs={{0,1},{1,0},{2,3},{3,2},{4,5},{5,4},{6,7},{7,6},{8,9},{9,8},{10,11... | collective-permute-start | bytes 2654216 | tf_op jit(solution)/shard_map/ppermute | solution.py:34
  164.8 15.9 %collective-permute-start.24 = (bf16[384,768]{1,0:T(8,128)(2,1)S(1)}, bf16[384,768]{1,0:T(8,128)(2,1)S(1)}, u32[]{:S(2)}, u32[]{:S(2)}) collective-permute-start(bf16[384,768]{1,0:T(8,128)(2,1)S(1)} %constant_dynamic-slice_fusion.6), channel_id=1, source_target_pairs={{0,8},{8,0},{16,24},{24,16},{1,9},{9,1},{17,25},{25,17},{2,10},{10... | collective-permute-start | bytes 1769480 | tf_op jit(solution)/shard_map/ppermute | solution.py:1191
  186.3 28.9 %collective-permute-start.30 = (bf16[192,2048]{1,0:T(8,128)(2,1)}, bf16[192,2048]{1,0:T(8,128)(2,1)}, u32[]{:S(2)}, u32[]{:S(2)}) collective-permute-start(bf16[192,2048]{1,0:T(8,128)(2,1)} %dynamic-slice_bitcast_fusion), channel_id=1, source_target_pairs={{0,1},{1,0},{2,3},{3,2},{4,5},{5,4},{6,7},{7,6},{8,9},{9,8},{10,11... | collective-permute-start | bytes 2359304 | tf_op jit(solution)/shard_map/ppermute | solution.py:34
  188.7 26.5 %collective-permute-start.28 = (bf16[1024,384]{1,0:T(8,128)(2,1)}, bf16[1024,384]{1,0:T(8,128)(2,1)}, u32[]{:S(2)}, u32[]{:S(2)}) collective-permute-start(bf16[1024,384]{1,0:T(8,128)(2,1)} %add_convert_fusion.2), channel_id=1, source_target_pairs={{0,4},{4,0},{1,5},{5,1},{2,6},{6,2},{3,7},{7,3},{8,12},{12,8},{9,1... | collective-permute-start | bytes 2359304 | tf_op jit(solution)/shard_map/ppermute | solution.py:34
  191.3 23.9 %collective-permute-start.29 = (bf16[192,768]{1,0:T(8,128)(2,1)}, bf16[192,768]{1,0:T(8,128)(2,1)}, u32[]{:S(2)}, u32[]{:S(2)}) collective-permute-start(bf16[192,768]{1,0:T(8,128)(2,1)} %constant_dynamic-slice_fusion.5), channel_id=1, source_target_pairs={{0,16},{16,0},{8,24},{24,8},{1,17},{17,1},{9,25},{25,9},{2,18},{18... | collective-permute-start | bytes 884744 | tf_op jit(solution)/shard_map/ppermute | solution.py:1194
  192.7 21.2 %collective-permute-start.32 = (bf16[192,256]{1,0:T(8,128)(2,1)S(1)}, bf16[192,256]{1,0:T(8,128)(2,1)S(1)}, u32[]{:S(2)}, u32[]{:S(2)}) collective-permute-start(bf16[192,256]{1,0:T(8,128)(2,1)S(1)} %copy-done.22), channel_id=1, source_target_pairs={{0,16},{16,0},{8,24},{24,8},{1,17},{17,1},{9,25},{25,9},{2,18},{18... | collective-permute-start | bytes 294920 | tf_op jit(solution)/shard_map/ppermute | solution.py:1069
  199.8 14.7 %collective-permute-start.33 = (bf16[192,256]{1,0:T(8,128)(2,1)S(1)}, bf16[192,256]{1,0:T(8,128)(2,1)S(1)}, u32[]{:S(2)}, u32[]{:S(2)}) collective-permute-start(bf16[192,256]{1,0:T(8,128)(2,1)S(1)} %copy-done.25), channel_id=1, source_target_pairs={{0,24},{24,0},{8,16},{16,8},{1,25},{25,1},{9,17},{17,9},{2,26},{26... | collective-permute-start | bytes 294920 | tf_op jit(solution)/shard_map/ppermute | solution.py:1069
  223.5 16.2 %collective-permute-start.36 = (bf16[96,2048]{1,0:T(8,128)(2,1)}, bf16[96,2048]{1,0:T(8,128)(2,1)}, u32[]{:S(2)}, u32[]{:S(2)}) collective-permute-start(bf16[96,2048]{1,0:T(8,128)(2,1)} %constant_dynamic-slice_fusion.4), channel_id=1, source_target_pairs={{0,8},{8,0},{16,24},{24,16},{1,9},{9,1},{17,25},{25,17},{2,10},{10... | collective-permute-start | bytes 1179656 | tf_op jit(solution)/shard_map/ppermute | solution.py:1191
  228.1 20.0 %collective-permute-start.38 = (bf16[384,256]{1,0:T(8,128)(2,1)}, bf16[384,256]{1,0:T(8,128)(2,1)S(1)}, u32[]{:S(2)}, u32[]{:S(2)}) collective-permute-start(bf16[384,256]{1,0:T(8,128)(2,1)} %copy-done.35), channel_id=1, source_target_pairs={{0,8},{8,0},{16,24},{24,16},{1,9},{9,1},{17,25},{25,17},{2,10},{10... | collective-permute-start | bytes 589832 | tf_op jit(solution)/shard_map/ppermute | solution.py:1069
  228.2 23.0 %collective-permute-start.39 = (bf16[384,256]{1,0:T(8,128)(2,1)}, bf16[384,256]{1,0:T(8,128)(2,1)S(1)}, u32[]{:S(2)}, u32[]{:S(2)}) collective-permute-start(bf16[384,256]{1,0:T(8,128)(2,1)} %copy-done.33), channel_id=1, source_target_pairs={{0,16},{16,0},{8,24},{24,8},{1,17},{17,1},{9,25},{25,9},{2,18},{18... | collective-permute-start | bytes 589832 | tf_op jit(solution)/shard_map/ppermute | solution.py:1069
  232.3 20.0 %collective-permute-start.40 = (bf16[384,256]{1,0:T(8,128)(2,1)}, bf16[384,256]{1,0:T(8,128)(2,1)S(1)}, u32[]{:S(2)}, u32[]{:S(2)}) collective-permute-start(bf16[384,256]{1,0:T(8,128)(2,1)} %copy-done.31), channel_id=1, source_target_pairs={{0,24},{24,0},{8,16},{16,8},{1,25},{25,1},{9,17},{17,9},{2,26},{26... | collective-permute-start | bytes 589832 | tf_op jit(solution)/shard_map/ppermute | solution.py:1069
  234.3 28.2 %collective-permute-start.42 = (bf16[96,768]{1,0:T(8,128)(2,1)S(1)}, bf16[96,768]{1,0:T(8,128)(2,1)S(1)}, u32[]{:S(2)}, u32[]{:S(2)}) collective-permute-start(bf16[96,768]{1,0:T(8,128)(2,1)S(1)} %add_convert_fusion.9), channel_id=1, source_target_pairs={{0,16},{16,0},{8,24},{24,8},{1,17},{17,1},{9,25},{25,9},{2,18},{18... | collective-permute-start | bytes 442376 | tf_op jit(solution)/shard_map/ppermute | solution.py:1194
  246.0 16.5 %collective-permute-start.41 = (bf16[48,2048]{1,0:T(8,128)(2,1)S(1)}, bf16[48,2048]{1,0:T(8,128)(2,1)S(1)}, u32[]{:S(2)}, u32[]{:S(2)}) collective-permute-start(bf16[48,2048]{1,0:T(8,128)(2,1)S(1)} %constant_dynamic-slice_fusion.2), channel_id=1, source_target_pairs={{0,16},{16,0},{8,24},{24,8},{1,17},{17,1},{9,25},{25,9},{2,18},{18... | collective-permute-start | bytes 589832 | tf_op jit(solution)/shard_map/ppermute | solution.py:1194
  248.2 36.6 %collective-permute-start.49 = (bf16[576,768]{1,0:T(8,128)(2,1)S(1)}, bf16[576,768]{1,0:T(8,128)(2,1)S(1)}, u32[]{:S(2)}, u32[]{:S(2)}) collective-permute-start(bf16[576,768]{1,0:T(8,128)(2,1)S(1)} %copy-done.29), channel_id=1, source_target_pairs={{0,2},{2,0},{1,3},{3,1},{4,6},{6,4},{5,7},{7,5},{8,10},{10,8},{9,1... | collective-permute-start | bytes 2654216 | tf_op jit(solution)/shard_map/ppermute | solution.py:34
  264.4 19.9 %collective-permute-start.46 = (bf16[208,640]{1,0:T(8,128)(2,1)S(1)}, bf16[208,640]{1,0:T(8,128)(2,1)S(1)}, u32[]{:S(2)}, u32[]{:S(2)}) collective-permute-start(bf16[208,640]{1,0:T(8,128)(2,1)S(1)} %add_convert_fusion.6), channel_id=1, source_target_pairs={{0,16},{16,0},{8,24},{24,8},{1,17},{17,1},{9,25},{25,9},{2,18},{18... | collective-permute-start | bytes 798728 | tf_op jit(solution)/shard_map/ppermute | solution.py:1194
  275.7 23.1 %collective-permute-start.48 = (bf16[384,768]{1,0:T(8,128)(2,1)S(1)}, bf16[384,768]{1,0:T(8,128)(2,1)S(1)}, u32[]{:S(2)}, u32[]{:S(2)}) collective-permute-start(bf16[384,768]{1,0:T(8,128)(2,1)S(1)} %bitcast.47), channel_id=1, source_target_pairs={{0,4},{4,0},{1,5},{5,1},{2,6},{6,2},{3,7},{7,3},{8,12},{12,8},{9,1... | collective-permute-start | bytes 1769480 | tf_op jit(solution)/shard_map/ppermute | solution.py:34
  284.4 14.5 %collective-permute-start.50 = (bf16[416,640]{1,0:T(8,128)(2,1)S(1)}, bf16[416,640]{1,0:T(8,128)(2,1)S(1)}, u32[]{:S(2)}, u32[]{:S(2)}) collective-permute-start(bf16[416,640]{1,0:T(8,128)(2,1)S(1)} %maximum_select_fusion.3), channel_id=1, source_target_pairs={{0,8},{8,0},{16,24},{24,16},{1,9},{9,1},{17,25},{25,17},{2,10},{10... | collective-permute-start | bytes 1597448 | tf_op jit(solution)/shard_map/ppermute | solution.py:1191
  284.7 21.2 %collective-permute-start.51 = (bf16[192,2048]{1,0:T(8,128)(2,1)S(1)}, bf16[192,2048]{1,0:T(8,128)(2,1)}, u32[]{:S(2)}, u32[]{:S(2)}) collective-permute-start(bf16[192,2048]{1,0:T(8,128)(2,1)S(1)} %maximum_select_fusion.1.refs_0_), channel_id=1, source_target_pairs={{0,4},{4,0},{1,5},{5,1},{2,6},{6,2},{3,7},{7,3},{8,12},{12,8},{9,1... | collective-permute-start | bytes 2359304 | tf_op jit(solution)/shard_map/ppermute | solution.py:34
  288.6 14.2 %collective-permute-start.52 = (bf16[384,768]{1,0:T(8,128)(2,1)S(1)}, bf16[384,768]{1,0:T(8,128)(2,1)S(1)}, u32[]{:S(2)}, u32[]{:S(2)}) collective-permute-start(bf16[384,768]{1,0:T(8,128)(2,1)S(1)} %bitcast.48), channel_id=1, source_target_pairs={{0,2},{2,0},{1,3},{3,1},{4,6},{6,4},{5,7},{7,5},{8,10},{10,8},{9,1... | collective-permute-start | bytes 1769480 | tf_op jit(solution)/shard_map/ppermute | solution.py:34
  (103 other events, 829.4 us)
